TPU v7x, 768 devices: a whole 4x8x12 slice. The times are simulated.
768 devices in a mesh: gx: 96 (over y_lo, z, core), gy: 8 (over x, y_hi).
Axes of the slice: x: 4, y: 8 (y_hi: 2, y_lo: 4; y = y_hi * 4 + y_lo), z: 12, core: 2. Of those that a mesh axis runs over, the one named last changes fastest.
Arguments:
- position: float32 [3, 192, 32, 128], P(None, 'gx', 'gy'), may hold values from 0 to 48, as said below
- velocity: float32 [3, 192, 32, 128], P(None, 'gx', 'gy'), may hold values from -12 to 12
- force_old: float32 [3, 192, 32, 128], P(None, 'gx', 'gy'), may hold values from -6 to 6
- counts: int32 [192, 32], P('gx', 'gy'), may hold values from 64 to 128
- density_coef: float32 [4], replicated, may hold values from 0.02 to 0.08
- pair_coef: float32 [4], replicated, may hold values from 0.5 to 2.5
- embed_coef: float32 [2], replicated, may hold values from 0.2 to 2
Outputs:
- position_new: float32 [3, 192, 32, 128], P(None, 'gx', 'gy')
- velocity_new: float32 [3, 192, 32, 128], P(None, 'gx', 'gy')
- force_new: float32 [3, 192, 32, 128], P(None, 'gx', 'gy')
- stress: float32 [6, 192, 32, 128], P(None, 'gx', 'gy')
Inputs may be any that keep to these rules, and one draw needn't show every extreme that they name: A block's live atoms occupy its first counts slots. `position`: coordinates stay within a margin of the atom's own cell block column.
All inputs are finite; a program needn't handle non-finite values.
Results may differ from a plain program's by a relative error of at most 0.0003.
Values sent between devices are 32-bit elements; how exact they have to be, the bound alone decides.
No kernel may reach another device: no remote copies, remote signals or barrier semaphores. Data moves between devices by JAX's collectives and lax.ppermute only.
A program may use at most 32 MiB of HBM per device.

v0:
```python
import math

import jax
import jax.numpy as jnp
from jax import lax
from jax.sharding import PartitionSpec as P

cutoff = 5.5
time_step = 0.004
inverse_mass = 151.83
atom_volume = 11.8
stress_pairs = ((0, 0), (1, 1), (2, 2), (0, 1), (0, 2), (1, 2))
offsets_half = ((0, 1), (1, -1), (1, 0), (1, 1))


def with_halo(shard, sides, width):
    for axis, dim in sides:
        count, length = (lax.axis_size(axis), shard.shape[dim])
        up = [(i, (i + 1) % count) for i in range(count)]
        down = [(j, i) for i, j in up]
        last = lax.slice_in_dim(shard, length - width, length, axis=dim)
        leading = lax.slice_in_dim(shard, 0, width, axis=dim)
        before = lax.ppermute(last, axis, up)
        after = lax.ppermute(leading, axis, down)
        shard = jnp.concatenate([before, shard, after], axis=dim)
    return shard


def shifted(block, axis, distance):
    devices = range(lax.axis_size(axis))
    route = [((i - distance) % len(devices), i) for i in devices]
    return lax.ppermute(block, axis, route)


def poly_value(weight, coeffs):
    nested = coeffs[0] + weight * (coeffs[1] + weight * (coeffs[2] + weight * coeffs[3]))
    return weight * weight * nested


def poly_slope(weight, coeffs):
    nested = coeffs[0] + weight * (coeffs[1] + weight * (coeffs[2] + weight * coeffs[3]))
    rising = coeffs[1] + weight * (2.0 * coeffs[2] + weight * (3.0 * coeffs[3]))
    return 2.0 * weight * nested + weight * weight * rising


def embed_slope(density, coeffs):
    return -0.5 * coeffs[0] / jnp.sqrt(1.0 + density) + 2.0 * coeffs[1] * density


def pair_weight(mine_pos, other_pos, shift_x, shift_y):
    shifts = jnp.array([shift_x * cutoff, shift_y * cutoff, 0.0], dtype=jnp.float32)
    separation = mine_pos[:, :, :, None] - other_pos[:, :, None, :] - shifts[:, None, None, None]
    square = jnp.sum(separation * separation, axis=0)
    weight = jnp.maximum(1.0 - square / (cutoff * cutoff), 0.0)
    return (separation, weight)


def make_mask(mine_live, other_live, same_block):
    pair_mask = mine_live[:, :, None] * other_live[:, None, :]
    if same_block:
        atom_count = mine_live.shape[1]
        rows_iota = lax.broadcasted_iota(jnp.int32, (atom_count, atom_count), 0)
        cols_iota = lax.broadcasted_iota(jnp.int32, (atom_count, atom_count), 1)
        pair_mask = pair_mask * (rows_iota != cols_iota).astype(jnp.float32)[None]
    return pair_mask


def tile_terms(mine_block, other_block, shift_x, shift_y, density_coef, pair_coef):
    separation, weight = pair_weight(mine_block[:3], other_block[:3], shift_x, shift_y)
    pair_mask = make_mask(mine_block[3], other_block[3], shift_x == 0 and shift_y == 0)
    strength = (
        (
            (mine_block[4][:, :, None] + other_block[4][:, None, :])
            * poly_slope(weight, density_coef)
            + poly_slope(weight, pair_coef)
        )
        * pair_mask
        * (2.0 / (cutoff * cutoff))
    )
    pair_force = strength[None] * separation
    products = jnp.stack(
        [separation[first] * pair_force[second] for first, second in stress_pairs]
    ) * (0.5 / atom_volume)
    return (pair_force, products)


def upper_frame(source):
    row_frame = with_halo(source, (("gy", 2),), 1)
    column = shifted(row_frame[:, 0:1], "gx", -1)
    return jnp.concatenate([row_frame, column], axis=1)


def return_partials(framed, width_x, width_y):
    returned = shifted(framed[:, width_x:], "gx", 1)
    row_frame = framed[:, :width_x].at[:, 0:1].add(returned)
    rim_parts = jnp.concatenate([row_frame[:, :, 0:1], row_frame[:, :, width_y + 1 :]], axis=2)
    arrived = with_halo(rim_parts, (("gy", 2),), 1)
    interior = row_frame[:, :, 1 : width_y + 1]
    interior = interior.at[:, :, 0].add(arrived[:, :, 0])
    return interior.at[:, :, width_y - 1].add(arrived[:, :, 3])


def frame_partials(own_sum, side_list, offsets):
    framed = jnp.pad(own_sum, ((0, 0), (0, 1), (1, 1), (0, 0)))
    for (shift_x, shift_y), side_part in zip(offsets, side_list):
        framed = framed + jnp.pad(
            side_part, ((0, 0), (shift_x, 1 - shift_x), (1 + shift_y, 1 - shift_y), (0, 0))
        )
    return framed


def grouped(framed, start_x, start_y, width_x, width_y, step_count):
    window = framed[:, start_x : start_x + width_x, start_y : start_y + width_y]
    channels, atom_count = (window.shape[0], window.shape[3])
    return window.reshape(channels, step_count, -1, atom_count).transpose(1, 0, 2, 3)


def ungroup(stacked, width_x, width_y):
    channels, atom_count = (stacked.shape[1], stacked.shape[3])
    return stacked.transpose(1, 0, 2, 3).reshape(channels, width_x, width_y, atom_count)


def density_sweep(mine_steps, other_steps, offsets, density_coef):

    def density_scan_step(carried, inputs):
        mine_block, other_blocks = inputs
        totals = jnp.zeros(mine_block.shape[1:], jnp.float32)
        side_sums = []
        for (shift_x, shift_y), other_block in zip(offsets, other_blocks):
            same_block = shift_x == 0 and shift_y == 0
            weight = pair_weight(mine_block[:3], other_block[:3], shift_x, shift_y)[1]
            values = make_mask(mine_block[3], other_block[3], same_block) * poly_value(
                weight, density_coef
            )
            totals = totals + jnp.sum(values, axis=2)
            if not same_block:
                side_sums.append(jnp.sum(values, axis=1)[None])
        return (carried, (totals[None], tuple(side_sums)))

    return lax.scan(
        density_scan_step, jnp.zeros((), jnp.float32), (mine_steps, tuple(other_steps))
    )[1]


def force_sweep(mine_steps, other_steps, offsets, density_coef, pair_coef):

    def force_scan_step(carried, inputs):
        mine_block, other_blocks = inputs
        totals = jnp.zeros((9,) + mine_block.shape[1:], jnp.float32)
        side_sums = []
        for (shift_x, shift_y), other_block in zip(offsets, other_blocks):
            same_block = shift_x == 0 and shift_y == 0
            pair_force, products = tile_terms(
                mine_block, other_block, shift_x, shift_y, density_coef, pair_coef
            )
            totals = totals + jnp.concatenate(
                [jnp.sum(pair_force, axis=3), jnp.sum(products, axis=3)], axis=0
            )
            if not same_block:
                side_sums.append(
                    jnp.concatenate(
                        [-jnp.sum(pair_force, axis=2), jnp.sum(products, axis=2)], axis=0
                    )
                )
        return (carried, (totals, tuple(side_sums)))

    return lax.scan(force_scan_step, jnp.zeros((), jnp.float32), (mine_steps, tuple(other_steps)))[
        1
    ]


def body(position, velocity, force_old, counts, density_coef, pair_coef, embed_coef):
    kick_scale = 0.5 * time_step * inverse_mass
    velocity_half = velocity + kick_scale * force_old
    position_new = position + time_step * velocity_half
    width_x, width_y, atom_count = position.shape[1:]
    alive_mask = (
        lax.broadcasted_iota(jnp.int32, (width_x, width_y, atom_count), 2) < counts[:, :, None]
    ).astype(jnp.float32)
    carried_data = jnp.concatenate([position_new, alive_mask[None]], axis=0)
    block_total = width_x * width_y
    step_count = block_total // math.gcd(block_total, 4)
    offsets = ((0, 0),) + offsets_half
    pos_frame = upper_frame(carried_data)
    mine_steps = grouped(pos_frame, 0, 1, width_x, width_y, step_count)
    other_steps = [
        grouped(pos_frame, shift_x, 1 + shift_y, width_x, width_y, step_count)
        for shift_x, shift_y in offsets
    ]
    totals, side_sums = density_sweep(mine_steps, other_steps, offsets, density_coef)
    partial_frame = frame_partials(
        ungroup(totals, width_x, width_y),
        [ungroup(side_part, width_x, width_y) for side_part in side_sums],
        offsets_half,
    )
    density = return_partials(partial_frame, width_x, width_y)[0]
    slopes = embed_slope(density, embed_coef)
    full_frame = jnp.concatenate([pos_frame, upper_frame(slopes[None])], axis=0)
    mine_steps = grouped(full_frame, 0, 1, width_x, width_y, step_count)
    other_steps = [
        grouped(full_frame, shift_x, 1 + shift_y, width_x, width_y, step_count)
        for shift_x, shift_y in offsets
    ]
    results, side_sums = force_sweep(mine_steps, other_steps, offsets, density_coef, pair_coef)
    partial_frame = frame_partials(
        ungroup(results, width_x, width_y),
        [ungroup(side_part, width_x, width_y) for side_part in side_sums],
        offsets_half,
    )
    combined = return_partials(partial_frame, width_x, width_y)
    forces = combined[:3]
    stress = combined[3:]
    velocity_new = velocity_half + kick_scale * forces
    return (position_new, velocity_new, forces, stress)


def solution(mesh):
    in_specs = (
        P(None, "gx", "gy", None),
        P(None, "gx", "gy", None),
        P(None, "gx", "gy", None),
        P("gx", "gy"),
        P(),
        P(),
        P(),
    )
    out_specs = (
        P(None, "gx", "gy", None),
        P(None, "gx", "gy", None),
        P(None, "gx", "gy", None),
        P(None, "gx", "gy", None),
    )
    return jax.shard_map(body, mesh=mesh, in_specs=in_specs, out_specs=out_specs, check_vma=False)
```

profile of v0, /device:TPU:6, one launch (start us, length us, event | category | flops | bytes accessed | tf_op | source)
XLA Modules:
  0.0 182.3 jit_solution(9527750463521335196)
XLA Ops:
  2.2 7.7 %collective-permute-start = (f32[4,2,1,128]{3,2,1,0:T(1,128)S(1)}, f32[4,2,1,128]{3,2,1,0:T(1,128)S(1)}, u32[]{:S(2)}, u32[]{:S(2)}) collective-permute-start(f32[4,2,1,128]{3,2,1,0:T(1,128)S(1)} %get-tuple-element.767), channel_id=1, source_target_pairs={{0,1},{1,2},{2,3},{3,4},{4,5},{5,6},{6,7},{7,0},{8,9},{9,10},{10,1... | collective-permute-start | bytes 12296 | tf_op jit(solution)/shard_map/ppermute | solution.py:23
  12.9 9.5 %collective-permute-done.1 = f32[4,2,1,128]{3,2,1,0:T(1,128)S(1)} collective-permute-done((f32[4,2,1,128]{3,2,1,0:T(1,128)S(1)}, f32[4,2,1,128]{3,2,1,0:T(1,128)S(1)}, u32[]{:S(2)}, u32[]{:S(2)}) %collective-permute-start.1) | collective-permute-done | bytes 4128 | tf_op jit(solution)/shard_map/ppermute | solution.py:24
  22.4 9.9 %collective-permute-start.2 = (f32[4,1,6,128]{3,2,1,0:T(8,128)S(1)}, f32[4,1,6,128]{3,2,1,0:T(8,128)S(1)}, u32[]{:S(2)}, u32[]{:S(2)}) collective-permute-start(f32[4,1,6,128]{3,2,1,0:T(8,128)S(1)} %pad_maximum_fusion.4), channel_id=1, source_target_pairs={{8,0},{16,8},{24,16},{32,24},{40,32},{48,40},{56,48},{64,56},{72,6... | collective-permute-start | bytes 36872 | tf_op jit(solution)/shard_map/ppermute | solution.py:32
  33.8 13.1 %while.47 = (s32[]{:T(128)}, f32[2,1,4,128]{3,0,2,1:T(2,128)S(1)}, f32[2,1,4,128]{3,0,2,1:T(2,128)S(1)}, f32[2,1,4,128]{3,0,2,1:T(2,128)S(1)}, f32[2,1,4,128]{3,...) while((s32[]{:T(128)}, f32[2,1,4,128]{3,0,2,1:T(2,128)S(1)}, ...), condition=%wide.region_15.16_spmd.clone, body=%wide.region_0.15_spmd.sunk.clone.sunk | while | flops 8353282 | bytes 3008813 | solution.py:140
  36.8 3.3 %fusion.87 = (f32[4,128]{1,0:T(4,128)S(1)}, f32[4,128]{1,0:T(4,128)S(1)}, f32[4,128]{1,0:T(4,128)S(1)}, f32[4,128]{1,0:T(4,128)S(1)}, f32[4,128]{1,0:T(4,128)S(1...) fusion(f32[]{:T(128)} %bitcast.246, f32[]{:T(128)} %bitcast.247, ...), kind=kLoop, calls=%fused_computation.22.clone.1 | loop fusion | flops 4910592 | bytes 1404944 | tf_op jit(solution)/shard_map/while/body/eval_jaxpr/reduce_sum | solution.py:137
  48.9 6.9 %collective-permute-done.3 = f32[1,1,6,128]{3,1,2,0:T(1,128)S(1)} collective-permute-done((f32[1,1,6,128]{3,1,2,0:T(1,128)S(1)}, f32[1,1,6,128]{3,1,2,0:T(1,128)S(1)}, u32[]{:S(2)}, u32[]{:S(2)}) %collective-permute-start.3) | collective-permute-done | bytes 3104 | tf_op jit(solution)/shard_map/ppermute | solution.py:32
  55.8 6.7 %collective-permute-start.4 = (f32[1,2,1,128]{3,1,2,0:T(2,128)S(1)}, f32[1,2,1,128]{3,1,2,0:T(2,128)S(1)}, u32[]{:S(2)}, u32[]{:S(2)}) collective-permute-start(f32[1,2,1,128]{3,1,2,0:T(2,128)S(1)} %get-tuple-element.772), channel_id=1, source_target_pairs={{0,1},{1,2},{2,3},{3,4},{4,5},{5,6},{6,7},{7,0},{8,9},{9,10},{10,1... | collective-permute-start | bytes 3080 | tf_op jit(solution)/shard_map/ppermute | solution.py:23
  64.4 3.9 %collective-permute-start.5 = (f32[1,2,1,128]{3,1,2,0:T(2,128)S(1)}, f32[1,2,1,128]{3,1,2,0:T(2,128)S(1)}, u32[]{:S(2)}, u32[]{:S(2)}) collective-permute-start(f32[1,2,1,128]{3,1,2,0:T(2,128)S(1)} %get-tuple-element.771), channel_id=1, source_target_pairs={{1,0},{2,1},{3,2},{4,3},{5,4},{6,5},{7,6},{0,7},{9,8},{10,9},{11,1... | collective-permute-start | bytes 3080 | tf_op jit(solution)/shard_map/ppermute | solution.py:24
  68.4 5.4 %collective-permute-done.5 = f32[1,2,1,128]{3,1,2,0:T(2,128)S(1)} collective-permute-done((f32[1,2,1,128]{3,1,2,0:T(2,128)S(1)}, f32[1,2,1,128]{3,1,2,0:T(2,128)S(1)}, u32[]{:S(2)}, u32[]{:S(2)}) %collective-permute-start.5) | collective-permute-done | bytes 1056 | tf_op jit(solution)/shard_map/ppermute | solution.py:24
  73.9 5.0 %collective-permute-start.6 = (f32[1,2,1,128]{3,2,1,0:T(1,128)S(1)}, f32[1,2,1,128]{3,2,1,0:T(1,128)S(1)}, u32[]{:S(2)}, u32[]{:S(2)}) collective-permute-start(f32[1,2,1,128]{3,2,1,0:T(1,128)S(1)} %get-tuple-element.773), channel_id=1, source_target_pairs={{0,1},{1,2},{2,3},{3,4},{4,5},{5,6},{6,7},{7,0},{8,9},{9,10},{10,1... | collective-permute-start | bytes 3080 | tf_op jit(solution)/shard_map/ppermute | solution.py:23
  78.9 5.6 %collective-permute-start.7 = (f32[1,2,1,128]{3,2,1,0:T(1,128)S(1)}, f32[1,2,1,128]{3,2,1,0:T(1,128)S(1)}, u32[]{:S(2)}, u32[]{:S(2)}) collective-permute-start(f32[1,2,1,128]{3,2,1,0:T(1,128)S(1)} %get-tuple-element.774), channel_id=1, source_target_pairs={{1,0},{2,1},{3,2},{4,3},{5,4},{6,5},{7,6},{0,7},{9,8},{10,9},{11,1... | collective-permute-start | bytes 3080 | tf_op jit(solution)/shard_map/ppermute | solution.py:24
  93.5 62.2 %while.48 = (s32[]{:T(128)}, f32[2,9,4,128]{3,2,0,1:T(4,128)S(1)}, f32[2,9,4,128]{3,2,0,1:T(4,128)S(1)}, f32[2,9,4,128]{3,2,0,1:T(4,128)S(1)}, f32[2,9,4,128]{3,...) while((s32[]{:T(128)}, f32[2,9,4,128]{3,2,0,1:T(4,128)S(1)}, ...), condition=%wide.region_40.41_spmd.clone, body=%wide.region_16.40_spmd.sunk.clone.sunk | while | flops 27648000 | bytes 45474684 | solution.py:167
  96.8 5.6 %multiply_multiply_fusion.13 = (f32[4,128,128]{2,1,0:T(8,128)S(1)}, f32[4,128,128]{2,1,0:T(8,128)S(1)}) fusion(f32[4,128,128]{2,1,0:T(8,128)S(1)} %get-tuple-element.1057, f32[4,128]{1,0:T(4,128)S(1)} %get-tuple-element.1058, f32[4,128]{1,0:T(4,128)S(1)} %get-tuple-element.1059, f32[4,128]{1,0:T(4,128)S(1)} %get-tuple-element.1060, ...), kind=kLoop, calls=%fused_computation.96.clone.1 | loop fusion | flops 4915200 | bytes 1122352 | tf_op jit(solution)/shard_map/while/body/eval_jaxpr/mul | solution.py:72
  103.6 5.3 %multiply_multiply_fusion.14 = f32[4,128,128]{2,1,0:T(8,128)S(1)} fusion(f32[4,128,128]{2,1,0:T(8,128)S(1)} %get-tuple-element.1076, f32[4,128]{1,0:T(4,128)S(1)} %get-tuple-element.1077, f32[4,128]{1,0:T(4,128)S(1)} %get-tuple-element.1078, f32[4,128]{1,0:T(4,128)S(1)} %get-tuple-element.1060, f32[]{:T(128)} %get-tuple-element.1223, ...), kind=kLoop, calls=%fused_computation.101.clone.1 | loop fusion | flops 2424832 | bytes 532528 | tf_op jit(solution)/shard_map/while/body/eval_jaxpr/mul | solution.py:72
  108.9 5.3 %multiply_multiply_fusion.15 = f32[4,128,128]{2,1,0:T(8,128)S(1)} fusion(f32[4,128,128]{2,1,0:T(8,128)S(1)} %get-tuple-element.1079, f32[4,128]{1,0:T(4,128)S(1)} %get-tuple-element.1080, f32[4,128]{1,0:T(4,128)S(1)} %get-tuple-element.1081, f32[4,128]{1,0:T(4,128)S(1)} %get-tuple-element.1060, f32[]{:T(128)} %get-tuple-element.1223, ...), kind=kLoop, calls=%fused_computation.106.clone.1 | loop fusion | flops 2424832 | bytes 532528 | tf_op jit(solution)/shard_map/while/body/eval_jaxpr/mul | solution.py:72
  114.2 5.3 %multiply_multiply_fusion.16 = f32[4,128,128]{2,1,0:T(8,128)S(1)} fusion(f32[4,128,128]{2,1,0:T(8,128)S(1)} %get-tuple-element.1082, f32[4,128]{1,0:T(4,128)S(1)} %get-tuple-element.1083, f32[4,128]{1,0:T(4,128)S(1)} %get-tuple-element.1084, f32[4,128]{1,0:T(4,128)S(1)} %get-tuple-element.1060, f32[]{:T(128)} %get-tuple-element.1223, ...), kind=kLoop, calls=%fused_computation.111.clone.1 | loop fusion | flops 2424832 | bytes 532528 | tf_op jit(solution)/shard_map/while/body/eval_jaxpr/mul | solution.py:72
  127.9 5.6 %multiply_multiply_fusion.13 = (f32[4,128,128]{2,1,0:T(8,128)S(1)}, f32[4,128,128]{2,1,0:T(8,128)S(1)}) fusion(f32[4,128,128]{2,1,0:T(8,128)S(1)} %get-tuple-element.1057, f32[4,128]{1,0:T(4,128)S(1)} %get-tuple-element.1058, f32[4,128]{1,0:T(4,128)S(1)} %get-tuple-element.1059, f32[4,128]{1,0:T(4,128)S(1)} %get-tuple-element.1060, ...), kind=kLoop, calls=%fused_computation.96.clone.1 | loop fusion | flops 4915200 | bytes 1122352 | tf_op jit(solution)/shard_map/while/body/eval_jaxpr/mul | solution.py:72
  134.7 5.3 %multiply_multiply_fusion.14 = f32[4,128,128]{2,1,0:T(8,128)S(1)} fusion(f32[4,128,128]{2,1,0:T(8,128)S(1)} %get-tuple-element.1076, f32[4,128]{1,0:T(4,128)S(1)} %get-tuple-element.1077, f32[4,128]{1,0:T(4,128)S(1)} %get-tuple-element.1078, f32[4,128]{1,0:T(4,128)S(1)} %get-tuple-element.1060, f32[]{:T(128)} %get-tuple-element.1223, ...), kind=kLoop, calls=%fused_computation.101.clone.1 | loop fusion | flops 2424832 | bytes 532528 | tf_op jit(solution)/shard_map/while/body/eval_jaxpr/mul | solution.py:72
  140.0 5.3 %multiply_multiply_fusion.15 = f32[4,128,128]{2,1,0:T(8,128)S(1)} fusion(f32[4,128,128]{2,1,0:T(8,128)S(1)} %get-tuple-element.1079, f32[4,128]{1,0:T(4,128)S(1)} %get-tuple-element.1080, f32[4,128]{1,0:T(4,128)S(1)} %get-tuple-element.1081, f32[4,128]{1,0:T(4,128)S(1)} %get-tuple-element.1060, f32[]{:T(128)} %get-tuple-element.1223, ...), kind=kLoop, calls=%fused_computation.106.clone.1 | loop fusion | flops 2424832 | bytes 532528 | tf_op jit(solution)/shard_map/while/body/eval_jaxpr/mul | solution.py:72
  145.3 5.3 %multiply_multiply_fusion.16 = f32[4,128,128]{2,1,0:T(8,128)S(1)} fusion(f32[4,128,128]{2,1,0:T(8,128)S(1)} %get-tuple-element.1082, f32[4,128]{1,0:T(4,128)S(1)} %get-tuple-element.1083, f32[4,128]{1,0:T(4,128)S(1)} %get-tuple-element.1084, f32[4,128]{1,0:T(4,128)S(1)} %get-tuple-element.1060, f32[]{:T(128)} %get-tuple-element.1223, ...), kind=kLoop, calls=%fused_computation.111.clone.1 | loop fusion | flops 2424832 | bytes 532528 | tf_op jit(solution)/shard_map/while/body/eval_jaxpr/mul | solution.py:72
  158.2 6.8 %collective-permute-done.9 = f32[9,1,6,128]{3,2,1,0:T(8,128)S(1)} collective-permute-done((f32[9,1,6,128]{3,2,1,0:T(8,128)S(1)}, f32[9,1,6,128]{3,2,1,0:T(8,128)S(1)}, u32[]{:S(2)}, u32[]{:S(2)}) %collective-permute-start.9) | collective-permute-done | bytes 27680 | tf_op jit(solution)/shard_map/ppermute | solution.py:32
  164.9 6.5 %collective-permute-start.10 = (f32[9,2,1,128]{3,2,1,0:T(1,128)S(1)}, f32[9,2,1,128]{3,2,1,0:T(1,128)S(1)}, u32[]{:S(2)}, u32[]{:S(2)}) collective-permute-start(f32[9,2,1,128]{3,2,1,0:T(1,128)S(1)} %get-tuple-element.758), channel_id=1, source_target_pairs={{0,1},{1,2},{2,3},{3,4},{4,5},{5,6},{6,7},{7,0},{8,9},{9,10},{10,1... | collective-permute-start | bytes 27656 | tf_op jit(solution)/shard_map/ppermute | solution.py:23
  171.5 4.1 %collective-permute-start.11 = (f32[9,2,1,128]{3,2,1,0:T(1,128)S(1)}, f32[9,2,1,128]{3,2,1,0:T(1,128)S(1)}, u32[]{:S(2)}, u32[]{:S(2)}) collective-permute-start(f32[9,2,1,128]{3,2,1,0:T(1,128)S(1)} %get-tuple-element.757), channel_id=1, source_target_pairs={{1,0},{2,1},{3,2},{4,3},{5,4},{6,5},{7,6},{0,7},{9,8},{10,9},{11,1... | collective-permute-start | bytes 27656 | tf_op jit(solution)/shard_map/ppermute | solution.py:24
  175.7 5.2 %collective-permute-done.11 = f32[9,2,1,128]{3,2,1,0:T(1,128)S(1)} collective-permute-done((f32[9,2,1,128]{3,2,1,0:T(1,128)S(1)}, f32[9,2,1,128]{3,2,1,0:T(1,128)S(1)}, u32[]{:S(2)}, u32[]{:S(2)}) %collective-permute-start.11) | collective-permute-done | bytes 9248 | tf_op jit(solution)/shard_map/ppermute | solution.py:24
  (256 shorter events, 46.8 us)
Async XLA Ops:
  2.1 91.2 %copy-start = (f32[3,2,4,128]{3,2,1,0:T(4,128)}, f32[3,2,4,128]{3,2,1,0:T(4,128)S(1)}, u32[]{:S(2)}) copy-start(f32[3,2,4,128]{3,2,1,0:T(4,128)S(1)} %multiply_add_fusion.1) | copy-start | bytes 36868
  2.2 10.7 %collective-permute-start = (f32[4,2,1,128]{3,2,1,0:T(1,128)S(1)}, f32[4,2,1,128]{3,2,1,0:T(1,128)S(1)}, u32[]{:S(2)}, u32[]{:S(2)}) collective-permute-start(f32[4,2,1,128]{3,2,1,0:T(1,128)S(1)} %get-tuple-element.767), channel_id=1, source_target_pairs={{0,1},{1,2},{2,3},{3,4},{4,5},{5,6},{6,7},{7,0},{8,9},{9,10},{10,1... | collective-permute-start | bytes 12296 | tf_op jit(solution)/shard_map/ppermute | solution.py:23
  9.9 12.5 %collective-permute-start.1 = (f32[4,2,1,128]{3,2,1,0:T(1,128)S(1)}, f32[4,2,1,128]{3,2,1,0:T(1,128)S(1)}, u32[]{:S(2)}, u32[]{:S(2)}) collective-permute-start(f32[4,2,1,128]{3,2,1,0:T(1,128)S(1)} %get-tuple-element.768), channel_id=1, source_target_pairs={{1,0},{2,1},{3,2},{4,3},{5,4},{6,5},{7,6},{0,7},{9,8},{10,9},{11,1... | collective-permute-start | bytes 12296 | tf_op jit(solution)/shard_map/ppermute | solution.py:24
  22.4 11.3 %collective-permute-start.2 = (f32[4,1,6,128]{3,2,1,0:T(8,128)S(1)}, f32[4,1,6,128]{3,2,1,0:T(8,128)S(1)}, u32[]{:S(2)}, u32[]{:S(2)}) collective-permute-start(f32[4,1,6,128]{3,2,1,0:T(8,128)S(1)} %pad_maximum_fusion.4), channel_id=1, source_target_pairs={{8,0},{16,8},{24,16},{32,24},{40,32},{48,40},{56,48},{64,56},{72,6... | collective-permute-start | bytes 36872 | tf_op jit(solution)/shard_map/ppermute | solution.py:32
  33.7 28.8 %copy-start.8 = (f32[2]{0:T(128)S(1)}, f32[2]{0:T(128)}, u32[]{:S(2)}) copy-start(f32[2]{0:T(128)} %param.39) | copy-start | bytes 28
  33.7 56.5 %copy-start.1 = (f32[4]{0:T(128)S(1)}, f32[4]{0:T(128)}, u32[]{:S(2)}) copy-start(f32[4]{0:T(128)} %param.38) | copy-start | bytes 52
  46.9 8.8 %collective-permute-start.3 = (f32[1,1,6,128]{3,1,2,0:T(1,128)S(1)}, f32[1,1,6,128]{3,1,2,0:T(1,128)S(1)}, u32[]{:S(2)}, u32[]{:S(2)}) collective-permute-start(f32[1,1,6,128]{3,1,2,0:T(1,128)S(1)} %pad_add_fusion.2), channel_id=1, source_target_pairs={{760,0},{0,8},{8,16},{16,24},{24,32},{32,40},{40,48},{48,56},{56,6... | collective-permute-start | bytes 9224 | tf_op jit(solution)/shard_map/ppermute | solution.py:32
  55.8 12.6 %collective-permute-start.4 = (f32[1,2,1,128]{3,1,2,0:T(2,128)S(1)}, f32[1,2,1,128]{3,1,2,0:T(2,128)S(1)}, u32[]{:S(2)}, u32[]{:S(2)}) collective-permute-start(f32[1,2,1,128]{3,1,2,0:T(2,128)S(1)} %get-tuple-element.772), channel_id=1, source_target_pairs={{0,1},{1,2},{2,3},{3,4},{4,5},{5,6},{6,7},{7,0},{8,9},{9,10},{10,1... | collective-permute-start | bytes 3080 | tf_op jit(solution)/shard_map/ppermute | solution.py:23
  64.4 9.4 %collective-permute-start.5 = (f32[1,2,1,128]{3,1,2,0:T(2,128)S(1)}, f32[1,2,1,128]{3,1,2,0:T(2,128)S(1)}, u32[]{:S(2)}, u32[]{:S(2)}) collective-permute-start(f32[1,2,1,128]{3,1,2,0:T(2,128)S(1)} %get-tuple-element.771), channel_id=1, source_target_pairs={{1,0},{2,1},{3,2},{4,3},{5,4},{6,5},{7,6},{0,7},{9,8},{10,9},{11,1... | collective-permute-start | bytes 3080 | tf_op jit(solution)/shard_map/ppermute | solution.py:24
  73.9 12.0 %collective-permute-start.6 = (f32[1,2,1,128]{3,2,1,0:T(1,128)S(1)}, f32[1,2,1,128]{3,2,1,0:T(1,128)S(1)}, u32[]{:S(2)}, u32[]{:S(2)}) collective-permute-start(f32[1,2,1,128]{3,2,1,0:T(1,128)S(1)} %get-tuple-element.773), channel_id=1, source_target_pairs={{0,1},{1,2},{2,3},{3,4},{4,5},{5,6},{6,7},{7,0},{8,9},{9,10},{10,1... | collective-permute-start | bytes 3080 | tf_op jit(solution)/shard_map/ppermute | solution.py:23
  78.9 9.4 %collective-permute-start.7 = (f32[1,2,1,128]{3,2,1,0:T(1,128)S(1)}, f32[1,2,1,128]{3,2,1,0:T(1,128)S(1)}, u32[]{:S(2)}, u32[]{:S(2)}) collective-permute-start(f32[1,2,1,128]{3,2,1,0:T(1,128)S(1)} %get-tuple-element.774), channel_id=1, source_target_pairs={{1,0},{2,1},{3,2},{4,3},{5,4},{6,5},{7,6},{0,7},{9,8},{10,9},{11,1... | collective-permute-start | bytes 3080 | tf_op jit(solution)/shard_map/ppermute | solution.py:24
  88.3 5.1 %collective-permute-start.8 = (f32[1,1,6,128]{3,2,1,0:T(8,128)S(1)}, f32[1,1,6,128]{3,2,1,0:T(8,128)S(1)}, u32[]{:S(2)}, u32[]{:S(2)}) collective-permute-start(f32[1,1,6,128]{3,2,1,0:T(8,128)S(1)} %pad_maximum_fusion.7), channel_id=1, source_target_pairs={{8,0},{16,8},{24,16},{32,24},{40,32},{48,40},{56,48},{64,56},{72,6... | collective-permute-start | bytes 9224 | tf_op jit(solution)/shard_map/ppermute | solution.py:32
  93.4 88.3 %copy-start.6 = (f32[3,2,4,128]{3,2,1,0:T(4,128)S(1)}, f32[3,2,4,128]{3,2,1,0:T(4,128)}, u32[]{:S(2)}) copy-start(f32[3,2,4,128]{3,2,1,0:T(4,128)} %param.34) | copy-start | bytes 36868
  93.4 88.2 %copy-start.7 = (f32[3,2,4,128]{3,2,1,0:T(4,128)S(1)}, f32[3,2,4,128]{3,2,1,0:T(4,128)}, u32[]{:S(2)}) copy-start(f32[3,2,4,128]{3,2,1,0:T(4,128)} %param.35) | copy-start | bytes 36868
  93.5 9.0 %copy-start.2 = (f32[3]{0:T(128)S(1)}, f32[3]{0:T(128)}, u32[]{:S(2)}) copy-start(f32[3]{0:T(128)} %get-tuple-element.1229) | copy-start | bytes 40 | tf_op jit(solution)/shard_map/while
  93.5 9.0 %copy-start.3 = (f32[3]{0:T(128)S(1)}, f32[3]{0:T(128)}, u32[]{:S(2)}) copy-start(f32[3]{0:T(128)} %get-tuple-element.1232) | copy-start | bytes 40 | tf_op jit(solution)/shard_map/while
  93.5 9.0 %copy-start.4 = (f32[3]{0:T(128)S(1)}, f32[3]{0:T(128)}, u32[]{:S(2)}) copy-start(f32[3]{0:T(128)} %get-tuple-element.1231) | copy-start | bytes 40 | tf_op jit(solution)/shard_map/while
  93.5 9.0 %copy-start.5 = (f32[3]{0:T(128)S(1)}, f32[3]{0:T(128)}, u32[]{:S(2)}) copy-start(f32[3]{0:T(128)} %get-tuple-element.1230) | copy-start | bytes 40 | tf_op jit(solution)/shard_map/while
  124.6 9.0 %copy-start.2 = (f32[3]{0:T(128)S(1)}, f32[3]{0:T(128)}, u32[]{:S(2)}) copy-start(f32[3]{0:T(128)} %get-tuple-element.1229) | copy-start | bytes 40 | tf_op jit(solution)/shard_map/while
  124.6 9.0 %copy-start.3 = (f32[3]{0:T(128)S(1)}, f32[3]{0:T(128)}, u32[]{:S(2)}) copy-start(f32[3]{0:T(128)} %get-tuple-element.1232) | copy-start | bytes 40 | tf_op jit(solution)/shard_map/while
  124.6 9.0 %copy-start.4 = (f32[3]{0:T(128)S(1)}, f32[3]{0:T(128)}, u32[]{:S(2)}) copy-start(f32[3]{0:T(128)} %get-tuple-element.1231) | copy-start | bytes 40 | tf_op jit(solution)/shard_map/while
  155.7 9.2 %collective-permute-start.9 = (f32[9,1,6,128]{3,2,1,0:T(8,128)S(1)}, f32[9,1,6,128]{3,2,1,0:T(8,128)S(1)}, u32[]{:S(2)}, u32[]{:S(2)}) collective-permute-start(f32[9,1,6,128]{3,2,1,0:T(8,128)S(1)} %slice.1005), channel_id=1, source_target_pairs={{760,0},{0,8},{8,16},{16,24},{24,32},{32,40},{40,48},{48,56},{56,6... | collective-permute-start | bytes 82952 | tf_op jit(solution)/shard_map/ppermute | solution.py:32
  164.9 10.7 %collective-permute-start.10 = (f32[9,2,1,128]{3,2,1,0:T(1,128)S(1)}, f32[9,2,1,128]{3,2,1,0:T(1,128)S(1)}, u32[]{:S(2)}, u32[]{:S(2)}) collective-permute-start(f32[9,2,1,128]{3,2,1,0:T(1,128)S(1)} %get-tuple-element.758), channel_id=1, source_target_pairs={{0,1},{1,2},{2,3},{3,4},{4,5},{5,6},{6,7},{7,0},{8,9},{9,10},{10,1... | collective-permute-start | bytes 27656 | tf_op jit(solution)/shard_map/ppermute | solution.py:23
  171.5 9.5 %collective-permute-start.11 = (f32[9,2,1,128]{3,2,1,0:T(1,128)S(1)}, f32[9,2,1,128]{3,2,1,0:T(1,128)S(1)}, u32[]{:S(2)}, u32[]{:S(2)}) collective-permute-start(f32[9,2,1,128]{3,2,1,0:T(1,128)S(1)} %get-tuple-element.757), channel_id=1, source_target_pairs={{1,0},{2,1},{3,2},{4,3},{5,4},{6,5},{7,6},{0,7},{9,8},{10,9},{11,1... | collective-permute-start | bytes 27656 | tf_op jit(solution)/shard_map/ppermute | solution.py:24
  (1 other events, 9.0 us)
where the time goes:
time: 184 us; the launch traced here: 182 us
  other arithmetic  68.8 us (37%)
  starting transfers between devices  58.7 us (32%)
  waiting for transfers between devices  37.6 us (20%)
  local copies, waits for them, and re-layouts  11.3 us (6%)
  between operations  4.82 us (3%)
    mul x8, other arithmetic, tile_terms(): ((mine_block[4][:, :, None] + other_block[4][:, None, :]) * poly_slope(we...  43 us
    ppermute x4, starting transfers between devices, with_halo(): before = lax.ppermute(last, axis, up)  26 us
    ppermute x4, waiting for transfers between devices, with_halo(): after = lax.ppermute(leading, axis, down)  22.6 us
    ppermute x4, starting transfers between devices, with_halo(): after = lax.ppermute(leading, axis, down)  16.5 us
    ppermute x4, starting transfers between devices, shifted(): return lax.ppermute(block, axis, route)  16.1 us
    ppermute x4, waiting for transfers between devices, shifted(): return lax.ppermute(block, axis, route)  15 us
    reduce_sum x2, other arithmetic, density_scan_step(): side_sums.append(jnp.sum(values, axis=1)[None])  6.6 us
    reduce_sum x4, other arithmetic, pair_weight(): square = jnp.sum(separation * separation, axis=0)  4.78 us
  transfers between devices with their start and end apart: 12, of which 7 were waited for; matrix products, arithmetic and copies ran while one was open for 1% of the time, Pallas kernels for 0%

commit v1 on v0

v1 whole, which is shorter than its diff:
```python
import functools

import jax
import jax.numpy as jnp
from jax import lax
from jax.experimental import pallas as pl
from jax.experimental.pallas import tpu as pltpu
from jax.sharding import PartitionSpec as P

cutoff = 5.5
time_step = 0.004
inverse_mass = 151.83
atom_volume = 11.8
kick_scale = 0.5 * time_step * inverse_mass
stress_pairs = ((0, 0), (1, 1), (2, 2), (0, 1), (0, 2), (1, 2))
SLOTS = 128
SLOTS_PER_A = 128.0 / 48.0
SLOT_LEAD = 1.5
FAR = 1.0e4
NONE = -1.0e6


def place_kernel(counts_ref, pos_ref, vel_ref, frc_ref, new_ref, half_ref, pay_ref, slot_ref):
    half = [vel_ref[c] + kick_scale * frc_ref[c] for c in range(3)]
    new = [pos_ref[c] + time_step * half[c] for c in range(3)]
    for c in range(3):
        half_ref[c] = half[c]
        new_ref[c] = new[c]
    rows = lax.broadcasted_iota(jnp.int32, (8, SLOTS), 0)
    lane_int = lax.broadcasted_iota(jnp.int32, (8, SLOTS), 1)
    lane = lane_int.astype(jnp.float32)
    count = jnp.zeros((8, SLOTS), jnp.int32)
    for b in range(8):
        count = jnp.where(rows == b, counts_ref[b], count)
    alive = lane_int < count
    wanted = new[2] * SLOTS_PER_A - SLOT_LEAD
    fine = jnp.clip(jnp.floor((wanted + 8.0) * 64.0), 0.0, 16383.0)
    key = jnp.where(alive, fine, 32768.0) * 128.0 + lane
    wanted = jnp.clip(jnp.floor(wanted), 0.0, 127.0)

    def column(values_t, b):
        return jnp.broadcast_to(values_t[:, b : b + 1], (SLOTS, SLOTS))

    key_t = key.T
    ranks = []
    for b in range(8):
        before = column(key_t, b) < key[b : b + 1]
        ranks.append(jnp.sum(jnp.where(before, 1.0, 0.0), axis=0, keepdims=True))
    rank = jnp.concatenate(ranks, axis=0)
    lead = jnp.where(alive, wanted - rank, NONE)
    lead_t = lead.T
    leads = []
    for b in range(8):
        before = column(key_t, b) < key[b : b + 1]
        leads.append(jnp.max(jnp.where(before, column(lead_t, b), NONE), axis=0, keepdims=True))
    slot = rank + jnp.maximum(lead, jnp.concatenate(leads, axis=0))
    slot = jnp.minimum(slot, 128.0 - count.astype(jnp.float32) + rank)
    slot = jnp.where(alive, slot, -1.0)
    slot_ref[...] = slot.astype(jnp.int32)
    slot_t = slot.T
    atom = lax.broadcasted_iota(jnp.int32, (SLOTS, SLOTS), 0).astype(jnp.float32)
    lanes = lax.broadcasted_iota(jnp.int32, (SLOTS, SLOTS), 1).astype(jnp.float32)
    owners = []
    for b in range(8):
        owners.append(
            jnp.max(jnp.where(column(slot_t, b) == lanes, atom, -1.0), axis=0, keepdims=True)
        )
    owner = jnp.concatenate(owners, axis=0)
    taken = owner >= 0.0
    index = jnp.maximum(owner, 0.0).astype(jnp.int32)
    for c in range(3):
        moved = jnp.take_along_axis(new[c], index, axis=1) * (1.0 / cutoff)
        pay_ref[c] = jnp.where(taken, moved, FAR if c == 0 else 0.0)


def pair_kernel(
    dens_ref, pair_ref, emb_ref, mid_ref, low_ref, high_ref, half_ref, slot_ref,
    vel_ref, frc_ref, str_ref,
    near, slopes, packs,
):
    for v in range(3):
        for x in range(6):
            for c in range(3):
                parts = []
                if v < 2:
                    parts.append(low_ref[c, x, v:2])
                parts.append(mid_ref[c, x])
                if v > 0:
                    parts.append(high_ref[c, x, 0:v])
                block = jnp.concatenate(parts, axis=0)
                if c == 1:
                    row = lax.broadcasted_iota(jnp.int32, (6, SLOTS), 0).astype(jnp.float32)
                    block = block + (row + (v - 3.5))
                elif c == 0:
                    block = block + (x - 2.5)
                near[v, c, 6 * x : 6 * x + 6] = block

    most, least = (None, None)
    lane = lax.broadcasted_iota(jnp.int32, (36, SLOTS), 1).astype(jnp.float32)
    for v in (0, 2):
        gap = lane - near[v, 2] * (cutoff * SLOTS_PER_A)
        there = near[v, 0] < 100.0
        high = jnp.where(there, gap, -1.0e6)
        low = jnp.where(there, gap, 1.0e6)
        most = high if most is None else jnp.maximum(most, high)
        least = low if least is None else jnp.minimum(least, low)
    spread = jnp.max(most) - jnp.min(least)
    reach = jnp.clip(spread + (cutoff * SLOTS_PER_A + 0.01), 0.0, 64.0).astype(jnp.int32)
    first = -reach
    last = jnp.minimum(reach, 63) + 1

    a = [dens_ref[k] for k in range(4)]
    p = [pair_ref[k] for k in range(4)]

    def load(v, u, c, m):
        start = 6 * (1 + u) + 8 * m
        return near[v + 1, c, start : start + 8]

    mine = [[load(0, 0, c, m) for c in range(3)] for m in range(3)]

    def density_step(d, totals):
        turn = lax.bitwise_and(d, 127)
        same = jnp.where(d == 0, 100.0, 0.0)
        totals = list(totals)
        for u in (-1, 0, 1):
            for v in (-1, 0, 1):
                for m in range(3):
                    square = None
                    for c in range(3):
                        other = pltpu.roll(load(v, u, c, m), turn, 1)
                        gap = mine[m][c] - other
                        square = gap * gap if square is None else square + gap * gap
                    if u == 0 and v == 0:
                        square = square + same
                    w = jnp.maximum(1.0 - square, 0.0)
                    value = a[0] + w * (a[1] + w * (a[2] + w * a[3]))
                    totals[m] = totals[m] + (w * w) * value
        return tuple(totals)

    zero = jnp.zeros((8, SLOTS), jnp.float32)
    totals = lax.fori_loop(first, last, density_step, (zero,) * 3)
    e0 = emb_ref[0]
    e1 = emb_ref[1]
    for m in range(3):
        slopes[8 * m : 8 * m + 8] = (-0.5 * e0) / jnp.sqrt(1.0 + totals[m]) + (2.0 * e1) * totals[m]

    for u in (-1, 0, 1):
        for v in (-1, 0, 1):
            k = 3 * (u + 1) + v + 1
            for side in range(2):
                for c in range(3):
                    start = 6 * (2 + side + u) + 1
                    packs[k, c, 4 * side : 4 * side + 4] = near[v + 1, c, start : start + 4]
                start = 6 * (1 + side + u) + 1 + v
                packs[k, 3, 4 * side : 4 * side + 4] = slopes[start : start + 4]

    own = [packs[4, c] for c in range(4)]
    gd = [(k + 2.0) * a[k] for k in range(4)]
    gp = [(k + 2.0) * p[k] for k in range(4)]

    def force_step(d, sums):
        turn = lax.bitwise_and(d, 127)
        same = jnp.where(d == 0, 100.0, 0.0)
        sums = list(sums)
        for k in range(9):
            gaps = [own[c] - pltpu.roll(packs[k, c], turn, 1) for c in range(3)]
            square = gaps[0] * gaps[0] + gaps[1] * gaps[1] + gaps[2] * gaps[2]
            if k == 4:
                square = square + same
            w = jnp.maximum(1.0 - square, 0.0)
            slope = own[3] + pltpu.roll(packs[k, 3], turn, 1)
            dens = gd[0] + w * (gd[1] + w * (gd[2] + w * gd[3]))
            pair = gp[0] + w * (gp[1] + w * (gp[2] + w * gp[3]))
            strength = w * (slope * dens + pair)
            pulls = [strength * gap for gap in gaps]
            for c in range(3):
                sums[c] = sums[c] + pulls[c]
            for t, (r, s) in enumerate(stress_pairs):
                sums[3 + t] = sums[3 + t] + gaps[r] * pulls[s]
        return tuple(sums)

    sums = lax.fori_loop(first, last, force_step, (zero,) * 9)
    slot = slot_ref[...]
    alive = slot >= 0
    index = jnp.maximum(slot, 0)

    def restored(values, scale):
        return jnp.where(alive, jnp.take_along_axis(values, index, axis=1) * scale, 0.0)

    for c in range(3):
        force = restored(sums[c], 2.0 / cutoff)
        frc_ref[c] = force
        vel_ref[c] = half_ref[c] + kick_scale * force
    for t in range(6):
        str_ref[t] = restored(sums[3 + t], 1.0 / atom_volume)


def shifted(block, axis, distance):
    count = lax.axis_size(axis)
    route = [(i, (i + distance) % count) for i in range(count)]
    return lax.ppermute(block, axis, route)


def body(position, velocity, force_old, counts, density_coef, pair_coef, embed_coef):
    shape = position.shape
    flat = (3, 8, SLOTS)
    vmem = pl.BlockSpec(memory_space=pltpu.VMEM)
    smem = pl.BlockSpec(memory_space=pltpu.SMEM)
    f32 = jnp.float32
    new, half, pay, slot = pl.pallas_call(
        place_kernel,
        in_specs=[smem, vmem, vmem, vmem],
        out_specs=[vmem] * 4,
        out_shape=[jax.ShapeDtypeStruct(flat, f32)] * 3
        + [jax.ShapeDtypeStruct((8, SLOTS), jnp.int32)],
        name="place",
    )(counts.reshape(8), position.reshape(flat), velocity.reshape(flat), force_old.reshape(flat))
    pay = pay.reshape(shape)
    before = shifted(pay, "gx", 1)
    after = shifted(pay, "gx", -1)
    mid = jnp.concatenate([before, pay, after], axis=1)
    low = shifted(mid[:, :, 2:], "gy", 1)
    high = shifted(mid[:, :, :2], "gy", -1)
    vel, frc, stress = pl.pallas_call(
        pair_kernel,
        in_specs=[smem] * 3 + [vmem] * 5,
        out_specs=[vmem] * 3,
        out_shape=[
            jax.ShapeDtypeStruct(flat, f32),
            jax.ShapeDtypeStruct(flat, f32),
            jax.ShapeDtypeStruct((6, 8, SLOTS), f32),
        ],
        scratch_shapes=[
            pltpu.VMEM((3, 3, 36, SLOTS), f32),
            pltpu.VMEM((24, SLOTS), f32),
            pltpu.VMEM((9, 4, 8, SLOTS), f32),
        ],
        name="pairs",
    )(density_coef, pair_coef, embed_coef, mid, low, high, half, slot)
    return (
        new.reshape(shape),
        vel.reshape(shape),
        frc.reshape(shape),
        stress.reshape((6,) + shape[1:]),
    )


def solution(mesh):
    grid = P(None, "gx", "gy", None)
    return jax.shard_map(
        body,
        mesh=mesh,
        in_specs=(grid, grid, grid, P("gx", "gy"), P(), P(), P()),
        out_specs=(grid, grid, grid, grid),
        check_vma=False,
    )
```

time: 184 us -> 62.9 us (0.34)
  the two profiles are of different devices: /device:TPU:6 before, /device:TPU:8 now
where the time goes in v1:
time: 62.9 us; the launch traced here: 62.5 us
  starting transfers between devices  27.7 us (44%)
  Pallas kernels  15.9 us (25%)
  waiting for transfers between devices  15.1 us (24%)
  local copies, waits for them, and re-layouts  2.46 us (4%)
  other arithmetic  0.72 us (1%)
  between operations  0.71 us (1%)
    ppermute x4, starting transfers between devices, shifted(): return lax.ppermute(block, axis, route)  27.7 us
    ppermute x4, waiting for transfers between devices, shifted(): return lax.ppermute(block, axis, route)  15.1 us
    pallas_call x1, Pallas kernels, body(): pl.pallas_call(pair_kernel, in_specs=[smem] * 3 + [vmem] * 5, out_specs=[...  13.4 us
    pallas_call x1, Pallas kernels, body(): pl.pallas_call(place_kernel, in_specs=[smem, vmem, vmem, vmem], out_specs...  2.45 us
    reshape x1, local copies, waits for them, and re-layouts, body(): counts.reshape(8)  1.27 us
  transfers between devices with their start and end apart: 4, of which 2 were waited for; matrix products, arithmetic and copies ran while one was open for 0% of the time, Pallas kernels for 0%

profile of v1, /device:TPU:8, one launch (start us, length us, event | category | flops | bytes accessed | tf_op | source)
XLA Modules:
  0.0 62.5 jit_solution(9687304598561951070)
XLA Ops:
  0.6 1.3 %reshape.35.counts_ref = s32[8]{0:T(128)} reshape(s32[2,4]{1,0:T(2,128)} %param.10) | data formatting | bytes 64 | tf_op jit(solution)/shard_map/reshape | solution.py:217
  1.9 2.5 %place.1 = (f32[3,8,128]{2,1,0:T(8,128)}, f32[3,8,128]{2,1,0:T(8,128)}, f32[3,8,128]{2,1,0:T(8,128)}, s32[8,128]{1,0:T(8,128)}) custom-call(s32[8]{0:T(128)} %reshape.35.counts_ref, f32[3,8,128]{2,1,0:T(8,128)} %bitcast.11, f32[3,8,128]{2,1,0:T(8,128)} %bitcast.12, f32[3,8,128]{2,1,0:T(8,128)} %bitcast.13), custom_call_target="tpu_custom_call" | custom-call | tf_op jit(solution)/shard_map/place/pallas_call | solution.py:210
  4.4 13.9 %collective-permute-start.1 = (f32[3,2,4,128]{3,2,1,0:T(4,128)}, f32[3,2,4,128]{3,2,1,0:T(4,128)S(1)}, u32[]{:S(2)}, u32[]{:S(2)}) collective-permute-start(f32[3,2,4,128]{3,2,1,0:T(4,128)} %bitcast.8), channel_id=1, source_target_pairs={{0,760},{8,0},{16,8},{24,16},{32,24},{40,32},{48,40},{56,48},{64,5... | collective-permute-start | bytes 36872 | tf_op jit(solution)/shard_map/ppermute | solution.py:201
  18.3 1.9 %collective-permute-start = (f32[3,2,4,128]{3,2,1,0:T(4,128)}, f32[3,2,4,128]{3,2,1,0:T(4,128)S(1)}, u32[]{:S(2)}, u32[]{:S(2)}) collective-permute-start(f32[3,2,4,128]{3,2,1,0:T(4,128)} %bitcast.9), channel_id=1, source_target_pairs={{0,8},{8,16},{16,24},{24,32},{32,40},{40,48},{48,56},{56,64},{64,7... | collective-permute-start | bytes 36872 | tf_op jit(solution)/shard_map/ppermute | solution.py:201
  20.2 0.0 collective-permute-done.1
  20.2 5.4 %collective-permute-done = f32[3,2,4,128]{3,2,1,0:T(4,128)S(1)} collective-permute-done((f32[3,2,4,128]{3,2,1,0:T(4,128)}, f32[3,2,4,128]{3,2,1,0:T(4,128)S(1)}, u32[]{:S(2)}, u32[]{:S(2)}) %collective-permute-start) | collective-permute-done | bytes 12320 | tf_op jit(solution)/shard_map/ppermute | solution.py:201
  25.6 0.7 %pad_maximum_fusion.mid_ref = f32[3,6,4,128]{3,2,1,0:T(4,128)S(1)} fusion(f32[3,2,4,128]{3,2,1,0:T(4,128)S(1)} %collective-permute-done.1, f32[3,2,4,128]{3,2,1,0:T(4,128)} %bitcast.10, f32[3,2,4,128]{3,2,1,0:T(4,128)S(1)} %collective-permute-done), kind=kLoop, calls=%fused_computation | loop fusion | flops 18432 | bytes 73728 | tf_op jit(solution)/shard_map/concatenate | solution.py:221
  26.3 0.0 copy-start
  26.3 0.6 copy-done
  26.9 9.9 %collective-permute-start.3 = (f32[3,6,2,128]{3,2,1,0:T(2,128)S(1)}, f32[3,6,2,128]{3,2,1,0:T(2,128)S(1)}, u32[]{:S(2)}, u32[]{:S(2)}) collective-permute-start(f32[3,6,2,128]{3,2,1,0:T(2,128)S(1)} %get-tuple-element.18), channel_id=1, source_target_pairs={{0,7},{1,0},{2,1},{3,2},{4,3},{5,4},{6,5},{7,6},{8,15},{9,8},{10,9... | collective-permute-start | bytes 55304 | tf_op jit(solution)/shard_map/ppermute | solution.py:201
  36.8 1.9 %collective-permute-start.2 = (f32[3,6,2,128]{3,2,1,0:T(2,128)S(1)}, f32[3,6,2,128]{3,2,1,0:T(2,128)S(1)}, u32[]{:S(2)}, u32[]{:S(2)}) collective-permute-start(f32[3,6,2,128]{3,2,1,0:T(2,128)S(1)} %get-tuple-element.19), channel_id=1, source_target_pairs={{0,1},{1,2},{2,3},{3,4},{4,5},{5,6},{6,7},{7,0},{8,9},{9,10},{10,1... | collective-permute-start | bytes 55304 | tf_op jit(solution)/shard_map/ppermute | solution.py:201
  38.8 0.0 collective-permute-done.3.high_ref
  38.8 0.0 copy-start.1
  38.8 9.7 %collective-permute-done.2.low_ref = f32[3,6,2,128]{3,2,1,0:T(2,128)S(1)} collective-permute-done((f32[3,6,2,128]{3,2,1,0:T(2,128)S(1)}, f32[3,6,2,128]{3,2,1,0:T(2,128)S(1)}, u32[]{:S(2)}, u32[]{:S(2)}) %collective-permute-start.2) | collective-permute-done | bytes 18464 | tf_op jit(solution)/shard_map/ppermute | solution.py:201
  48.5 0.0 copy-start.2
  48.5 0.0 copy-done.1
  48.5 0.6 copy-done.2
  49.1 13.4 %pairs.1 = (f32[3,8,128]{2,1,0:T(8,128)}, f32[3,8,128]{2,1,0:T(8,128)}, f32[6,8,128]{2,1,0:T(8,128)}) custom-call(f32[4]{0:T(128)} %dens_ref.1, f32[4]{0:T(128)} %pair_ref.1, f32[2]{0:T(128)} %emb_ref.1, f32[3,6,4,128]{3,2,1,0:T(4,128)} %copy-done, f32[3,6,2,128]{3,2,1,0:T(2,128)} %copy-done.2, f32[3,6,2,128]{3,2,1,0:T(2,128)} %copy-done.1, ...), custom_call_target="tpu_custom_call" | custom-call | tf_op jit(solution)/shard_map/pairs/pallas_call | solution.py:224
  (1 shorter events, 0.0 us)
Async XLA Ops:
  4.4 15.8 %collective-permute-start.1 = (f32[3,2,4,128]{3,2,1,0:T(4,128)}, f32[3,2,4,128]{3,2,1,0:T(4,128)S(1)}, u32[]{:S(2)}, u32[]{:S(2)}) collective-permute-start(f32[3,2,4,128]{3,2,1,0:T(4,128)} %bitcast.8), channel_id=1, source_target_pairs={{0,760},{8,0},{16,8},{24,16},{32,24},{40,32},{48,40},{56,48},{64,5... | collective-permute-start | bytes 36872 | tf_op jit(solution)/shard_map/ppermute | solution.py:201
  18.3 7.3 %collective-permute-start = (f32[3,2,4,128]{3,2,1,0:T(4,128)}, f32[3,2,4,128]{3,2,1,0:T(4,128)S(1)}, u32[]{:S(2)}, u32[]{:S(2)}) collective-permute-start(f32[3,2,4,128]{3,2,1,0:T(4,128)} %bitcast.9), channel_id=1, source_target_pairs={{0,8},{8,16},{16,24},{24,32},{32,40},{40,48},{48,56},{56,64},{64,7... | collective-permute-start | bytes 36872 | tf_op jit(solution)/shard_map/ppermute | solution.py:201
  26.3 0.6 copy-start
  26.9 11.9 %collective-permute-start.3 = (f32[3,6,2,128]{3,2,1,0:T(2,128)S(1)}, f32[3,6,2,128]{3,2,1,0:T(2,128)S(1)}, u32[]{:S(2)}, u32[]{:S(2)}) collective-permute-start(f32[3,6,2,128]{3,2,1,0:T(2,128)S(1)} %get-tuple-element.18), channel_id=1, source_target_pairs={{0,7},{1,0},{2,1},{3,2},{4,3},{5,4},{6,5},{7,6},{8,15},{9,8},{10,9... | collective-permute-start | bytes 55304 | tf_op jit(solution)/shard_map/ppermute | solution.py:201
  36.8 11.7 %collective-permute-start.2 = (f32[3,6,2,128]{3,2,1,0:T(2,128)S(1)}, f32[3,6,2,128]{3,2,1,0:T(2,128)S(1)}, u32[]{:S(2)}, u32[]{:S(2)}) collective-permute-start(f32[3,6,2,128]{3,2,1,0:T(2,128)S(1)} %get-tuple-element.19), channel_id=1, source_target_pairs={{0,1},{1,2},{2,3},{3,4},{4,5},{5,6},{6,7},{7,0},{8,9},{9,10},{10,1... | collective-permute-start | bytes 55304 | tf_op jit(solution)/shard_map/ppermute | solution.py:201
  38.8 9.7 %copy-start.1 = (f32[3,6,2,128]{3,2,1,0:T(2,128)}, f32[3,6,2,128]{3,2,1,0:T(2,128)S(1)}, u32[]{:S(2)}) copy-start(f32[3,6,2,128]{3,2,1,0:T(2,128)S(1)} %collective-permute-done.3.high_ref) | copy-start | bytes 55300
  48.5 0.6 copy-start.2

commit v2 on v1

v2 whole, which is shorter than its diff:
```python
import functools

import jax
import jax.numpy as jnp
from jax import lax
from jax.experimental import pallas as pl
from jax.experimental.pallas import tpu as pltpu
from jax.sharding import PartitionSpec as P

cutoff = 5.5
time_step = 0.004
inverse_mass = 151.83
atom_volume = 11.8
kick_scale = 0.5 * time_step * inverse_mass
stress_pairs = ((0, 0), (1, 1), (2, 2), (0, 1), (0, 2), (1, 2))
SLOTS = 128
SLOTS_PER_A = 128.0 / 48.0
SLOT_LEAD = 1.5
FAR = 1.0e4
NONE = -1.0e6
GRANT = 8 * 2**20


def place_kernel(counts_ref, pos_ref, vel_ref, frc_ref, new_ref, half_ref, pay_ref, slot_ref):
    half = [vel_ref[c] + kick_scale * frc_ref[c] for c in range(3)]
    new = [pos_ref[c] + time_step * half[c] for c in range(3)]
    for c in range(3):
        half_ref[c] = half[c]
        new_ref[c] = new[c]
    rows = lax.broadcasted_iota(jnp.int32, (8, SLOTS), 0)
    lane_int = lax.broadcasted_iota(jnp.int32, (8, SLOTS), 1)
    lane = lane_int.astype(jnp.float32)
    count = jnp.zeros((8, SLOTS), jnp.int32)
    for b in range(8):
        count = jnp.where(rows == b, counts_ref[b // 4, b % 4], count)
    alive = lane_int < count
    wanted = new[2] * SLOTS_PER_A - SLOT_LEAD
    fine = jnp.clip(jnp.floor((wanted + 8.0) * 64.0), 0.0, 16383.0)
    key = jnp.where(alive, fine, 32768.0) * 128.0 + lane
    wanted = jnp.clip(jnp.floor(wanted), 0.0, 127.0)

    def column(values_t, b):
        return jnp.broadcast_to(values_t[:, b : b + 1], (SLOTS, SLOTS))

    key_t = key.T
    ranks = []
    for b in range(8):
        before = column(key_t, b) < key[b : b + 1]
        ranks.append(jnp.sum(jnp.where(before, 1.0, 0.0), axis=0, keepdims=True))
    rank = jnp.concatenate(ranks, axis=0)
    lead = jnp.where(alive, wanted - rank, NONE)
    lead_t = lead.T
    leads = []
    for b in range(8):
        before = column(key_t, b) < key[b : b + 1]
        leads.append(jnp.max(jnp.where(before, column(lead_t, b), NONE), axis=0, keepdims=True))
    slot = rank + jnp.maximum(lead, jnp.concatenate(leads, axis=0))
    slot = jnp.minimum(slot, 128.0 - count.astype(jnp.float32) + rank)
    slot = jnp.where(alive, slot, -1.0)
    slot_ref[...] = slot.astype(jnp.int32)
    slot_t = slot.T
    atom = lax.broadcasted_iota(jnp.int32, (SLOTS, SLOTS), 0).astype(jnp.float32)
    lanes = lax.broadcasted_iota(jnp.int32, (SLOTS, SLOTS), 1).astype(jnp.float32)
    owners = []
    for b in range(8):
        owners.append(
            jnp.max(jnp.where(column(slot_t, b) == lanes, atom, -1.0), axis=0, keepdims=True)
        )
    owner = jnp.concatenate(owners, axis=0)
    taken = owner >= 0.0
    index = jnp.maximum(owner, 0.0).astype(jnp.int32)
    for c in range(3):
        moved = jnp.take_along_axis(new[c], index, axis=1) * (1.0 / cutoff)
        pay_ref[c] = jnp.where(taken, moved, FAR if c == 0 else 0.0)


def reach_of(boxes):
    most, least = (None, None)
    for far, height in boxes:
        lane = lax.broadcasted_iota(jnp.int32, height.shape, 1).astype(jnp.float32)
        gap = lane - height * (cutoff * SLOTS_PER_A)
        there = far < 100.0
        high = jnp.max(jnp.where(there, gap, -1.0e6))
        low = jnp.min(jnp.where(there, gap, 1.0e6))
        most = high if most is None else jnp.maximum(most, high)
        least = low if least is None else jnp.minimum(least, low)
    reach = most - least + (cutoff * SLOTS_PER_A + 0.01)
    return jnp.clip(reach, 0.0, 64.0).astype(jnp.int32)


def offsets_loop(reach, source, turned, step, start):
    rows = source.shape[0]

    def turn(d, ref):
        by = lax.bitwise_and(-d, SLOTS - 1)
        for r in range(0, rows, 8):
            ref[r : r + 8] = pltpu.roll(source[r : r + 8], by, 1)

    def pair(i, carry):
        d = 2 * i - reach
        turn(d + 1, turned.at[1])
        carry = step(d, turned.at[0], carry)
        turn(d + 2, turned.at[0])
        return step(d + 1, turned.at[1], carry)

    turn(-reach, turned.at[0])
    return lax.fori_loop(0, jnp.minimum(reach + 1, SLOTS // 2), pair, start)


def density_term(square, a):
    w = jnp.maximum(1.0 - square, 0.0)
    value = a[0] + w * (a[1] + w * (a[2] + w * a[3]))
    return (w * w) * value


def square_of(mine, others):
    gaps = [m - o for m, o in zip(mine, others)]
    return gaps[0] * gaps[0] + gaps[1] * gaps[1] + gaps[2] * gaps[2]


def early_kernel(dens_ref, pair_ref, emb_ref, mid_ref, sum_ref, coef_ref, source, turned):
    for k in range(4):
        coef_ref[k : k + 1] = jnp.full((1, SLOTS), dens_ref[k], jnp.float32)
        coef_ref[4 + k : 5 + k] = jnp.full((1, SLOTS), pair_ref[k], jnp.float32)
    for k in range(2):
        coef_ref[8 + k : 9 + k] = jnp.full((1, SLOTS), emb_ref[k], jnp.float32)
    boxes = []
    for x in range(6):
        boxes.append((mid_ref[0, x], mid_ref[2, x]))
        for v in range(3):
            for c in range(3):
                base = 24 * (3 * v + c) + 4 * x
                low = max(0, 1 - v)
                high = min(4, 5 - v)
                block = mid_ref[c, x, low + v - 1 : high + v - 1]
                row = lax.broadcasted_iota(jnp.int32, block.shape, 0).astype(jnp.float32)
                block = block + (x - 2.5, row + (low + v - 2.5), 0.0)[c]
                source[base + low : base + high] = block
                for edge in (0,) * low + (3,) * (4 - high):
                    source[base + edge : base + edge + 1] = jnp.full((1, SLOTS), FAR, jnp.float32)
    a = [dens_ref[k] for k in range(4)]

    def rows_of(ref, u, v, c, m):
        start = 24 * (3 * (v + 1) + c) + 4 * (1 + u) + 8 * m
        return ref[start : start + 8]

    mine = [[rows_of(source, 0, 0, c, m) for c in range(3)] for m in range(2)]

    def step(d, ref, totals):
        same = jnp.where(d == 0, 100.0, 0.0)
        totals = list(totals)
        for u in (-1, 0, 1):
            for v in (-1, 0, 1):
                for m in range(2):
                    square = square_of(mine[m], [rows_of(ref, u, v, c, m) for c in range(3)])
                    if u == 0 and v == 0:
                        square = square + same
                    totals[m] = totals[m] + density_term(square, a)
        return tuple(totals)

    zero = jnp.zeros((8, SLOTS), jnp.float32)
    totals = offsets_loop(reach_of(boxes), source, turned, step, (zero, zero))
    for m in range(2):
        sum_ref[8 * m : 8 * m + 8] = totals[m]


def late_kernel(
    mid_ref, low_ref, high_ref, half_ref, slot_ref, sum_ref, coef_ref,
    vel_ref, frc_ref, str_ref,
    rims, rims_turned, edges, slopes, packs, packs_turned,
):
    f32 = jnp.float32

    def block_row(c, x, y):
        if y < 2:
            values = low_ref[c, x, y : y + 1]
        elif y < 6:
            values = mid_ref[c, x, y - 2 : y - 1]
        else:
            values = high_ref[c, x, y - 6 : y - 5]
        return values + (x - 2.5, y - 3.5, 0.0)[c]

    for v in range(3):
        for c in range(3):
            for x in range(6):
                for s in range(2):
                    row = 12 * (3 * v + c) + 2 * x + s
                    rims[row : row + 1] = block_row(c, x, (1, 6)[s] + v - 1)
    boxes = []
    for x in range(6):
        boxes.append((mid_ref[0, x], mid_ref[2, x]))
        boxes.append((low_ref[0, x], low_ref[2, x]))
        boxes.append((high_ref[0, x], high_ref[2, x]))
    reach = reach_of(boxes)

    def coef(k):
        return jnp.broadcast_to(coef_ref[k : k + 1], (8, SLOTS))

    a = [coef(k) for k in range(4)]
    p = [coef(4 + k) for k in range(4)]

    def rim(ref, u, v, c):
        start = 12 * (3 * (v + 1) + c) + 2 * (1 + u)
        return ref[start : start + 8]

    outer = [rim(rims, 0, 0, c) for c in range(3)]
    for c in range(3):
        for x in range(4):
            for s in range(2):
                edges[c, 2 * x + s : 2 * x + s + 1] = block_row(c, x + 1, (2, 5)[s])
    inner = [edges[c] for c in range(3)]

    def density_step(d, ref, totals):
        same = jnp.where(d == 0, 100.0, 0.0)
        out, inn = totals
        for u in (-1, 0, 1):
            for v in (-1, 0, 1):
                others = [rim(ref, u, v, c) for c in range(3)]
                square = square_of(outer, others)
                if u == 0 and v == 0:
                    square = square + same
                out = out + density_term(square, a)
                if v == 0:
                    inn = inn + density_term(square_of(inner, others), a)
        return (out, inn)

    zero = jnp.zeros((8, SLOTS), f32)
    out, inn = offsets_loop(reach, rims, rims_turned, density_step, (zero, zero))
    edges[0] = out
    edges[1] = inn
    for x in range(4):
        for s in range(2):
            row = 2 * x + s
            slopes[6 * x + 5 * s : 6 * x + 5 * s + 1] = edges[0, row : row + 1]
            mine = 4 * x + 3 * s
            slopes[6 * x + 3 * s + 1 : 6 * x + 3 * s + 2] = (
                sum_ref[mine : mine + 1] + edges[1, row : row + 1]
            )
        slopes[6 * x + 2 : 6 * x + 4] = sum_ref[4 * x + 1 : 4 * x + 3]
    for m in range(3):
        total = slopes[8 * m : 8 * m + 8]
        slopes[8 * m : 8 * m + 8] = (-0.5 * coef(8)) / jnp.sqrt(1.0 + total) + (
            2.0 * coef(9)
        ) * total

    for u in (-1, 0, 1):
        for v in (-1, 0, 1):
            k = 3 * (u + 1) + v + 1
            for s in range(2):
                x = 2 + s + u
                for c in range(3):
                    base = 8 * (4 * k + c) + 4 * s
                    for y in range(2 + v, 6 + v):
                        if y in (1, 6):
                            packs[base + y - 2 - v : base + y - 1 - v] = block_row(c, x, y)
                    first = max(2, 2 + v)
                    last = min(6, 6 + v)
                    block = mid_ref[c, x, first - 2 : last - 2]
                    row = lax.broadcasted_iota(jnp.int32, block.shape, 0).astype(f32)
                    block = block + (x - 2.5, row + (first - 3.5), 0.0)[c]
                    packs[base + first - 2 - v : base + last - 2 - v] = block
                base = 8 * (4 * k + 3) + 4 * s
                start = 6 * (x - 1) + 1 + v
                packs[base : base + 4] = slopes[start : start + 4]

    def member(ref, k, c):
        return ref[8 * (4 * k + c) : 8 * (4 * k + c) + 8]

    own = [member(packs, 4, c) for c in range(4)]
    gd = [(k + 2.0) * a[k] for k in range(4)]
    gp = [(k + 2.0) * p[k] for k in range(4)]

    def force_step(d, ref, sums):
        same = jnp.where(d == 0, 100.0, 0.0)
        sums = list(sums)
        for k in range(9):
            gaps = [own[c] - member(ref, k, c) for c in range(3)]
            square = gaps[0] * gaps[0] + gaps[1] * gaps[1] + gaps[2] * gaps[2]
            if k == 4:
                square = square + same
            w = jnp.maximum(1.0 - square, 0.0)
            slope = own[3] + member(ref, k, 3)
            dens = gd[0] + w * (gd[1] + w * (gd[2] + w * gd[3]))
            pair = gp[0] + w * (gp[1] + w * (gp[2] + w * gp[3]))
            strength = w * (slope * dens + pair)
            pulls = [strength * gap for gap in gaps]
            for c in range(3):
                sums[c] = sums[c] + pulls[c]
            for t, (r, s) in enumerate(stress_pairs):
                sums[3 + t] = sums[3 + t] + gaps[r] * pulls[s]
        return tuple(sums)

    sums = offsets_loop(reach, packs, packs_turned, force_step, (zero,) * 9)
    slot = slot_ref[...]
    alive = slot >= 0
    index = jnp.maximum(slot, 0)

    def restored(values, scale):
        return jnp.where(alive, jnp.take_along_axis(values, index, axis=1) * scale, 0.0)

    for c in range(3):
        force = restored(sums[c], 2.0 / cutoff)
        frc_ref[c] = force
        vel_ref[c] = half_ref[c] + kick_scale * force
    for t in range(6):
        str_ref[t] = restored(sums[3 + t], 1.0 / atom_volume)


def shifted(block, axis, distance):
    count = lax.axis_size(axis)
    route = [(i, (i + distance) % count) for i in range(count)]
    return lax.ppermute(block, axis, route)


def body(position, velocity, force_old, counts, density_coef, pair_coef, embed_coef):
    shape = position.shape
    flat = (3, 8, SLOTS)
    vmem = pl.BlockSpec(memory_space=pltpu.VMEM)
    smem = pl.BlockSpec(memory_space=pltpu.SMEM)
    f32 = jnp.float32
    new, half, pay, slot = pl.pallas_call(
        place_kernel,
        in_specs=[smem, vmem, vmem, vmem],
        out_specs=[vmem] * 4,
        out_shape=[jax.ShapeDtypeStruct(flat, f32)] * 3
        + [jax.ShapeDtypeStruct((8, SLOTS), jnp.int32)],
        compiler_params=pltpu.CompilerParams(vmem_limit_bytes=GRANT),
        name="place",
    )(counts, position.reshape(flat), velocity.reshape(flat), force_old.reshape(flat))
    pay = pay.reshape(shape)
    after = shifted(pay, "gx", -1)
    before = shifted(pay, "gx", 1)
    mid = jnp.concatenate([before, pay, after], axis=1)
    high = shifted(mid[:, :, :2], "gy", -1)
    low = shifted(mid[:, :, 2:], "gy", 1)
    total, coefs = pl.pallas_call(
        early_kernel,
        in_specs=[smem] * 3 + [vmem],
        out_specs=[vmem] * 2,
        out_shape=[jax.ShapeDtypeStruct((16, SLOTS), f32)] * 2,
        scratch_shapes=[pltpu.VMEM((216, SLOTS), f32), pltpu.VMEM((2, 216, SLOTS), f32)],
        cost_estimate=pl.CostEstimate(flops=12000000, bytes_accessed=60000, transcendentals=0),
        compiler_params=pltpu.CompilerParams(vmem_limit_bytes=GRANT),
        name="early",
    )(density_coef, pair_coef, embed_coef, mid)
    vel, frc, stress = pl.pallas_call(
        late_kernel,
        in_specs=[vmem] * 7,
        out_specs=[vmem] * 3,
        out_shape=[
            jax.ShapeDtypeStruct(flat, f32),
            jax.ShapeDtypeStruct(flat, f32),
            jax.ShapeDtypeStruct((6, 8, SLOTS), f32),
        ],
        scratch_shapes=[
            pltpu.VMEM((112, SLOTS), f32),
            pltpu.VMEM((2, 112, SLOTS), f32),
            pltpu.VMEM((3, 8, SLOTS), f32),
            pltpu.VMEM((24, SLOTS), f32),
            pltpu.VMEM((288, SLOTS), f32),
            pltpu.VMEM((2, 288, SLOTS), f32),
        ],
        compiler_params=pltpu.CompilerParams(vmem_limit_bytes=GRANT),
        name="late",
    )(mid, low, high, half, slot, total, coefs)
    return (
        new.reshape(shape),
        vel.reshape(shape),
        frc.reshape(shape),
        stress.reshape((6,) + shape[1:]),
    )


def solution(mesh):
    grid = P(None, "gx", "gy", None)
    return jax.shard_map(
        body,
        mesh=mesh,
        in_specs=(grid, grid, grid, P("gx", "gy"), P(), P(), P()),
        out_specs=(grid, grid, grid, grid),
        check_vma=False,
    )
```

time: 62.9 us -> 55.5 us (0.88)
  waiting for transfers between devices: 15.1 us -> 11.4 us
  Pallas kernels: 15.9 us -> 12.3 us
  other arithmetic: 0.72 us -> 0.01 us
    ppermute x4, waiting for transfers between devices: 15.1 us -> 11.4 us  [shifted(): return lax.ppermute(block, axis, route)]
    pallas_call x1 -> x2, Pallas kernels: 13.4 us -> 10.2 us  [the longest x1 6.72 us: body(): pl.pallas_call(late_kernel, in_specs=[vmem] * 7, out_specs=[vmem] * 3, ou...]
    unnamed x6 -> x14, local copies, waits for them, and re-layouts: 1.17 us -> 2.81 us
    reshape x1 -> x0, local copies, waits for them, and re-layouts: 1.27 us -> none  [body(): counts.reshape(8)]
    concatenate x1, other arithmetic: 0.72 us -> 0.01 us  [body(): mid = jnp.concatenate([before, pay, after], axis=1)]
  transfers between devices with their start and end apart: 4 -> 4, of which waited for: 2 -> 2; matrix products, arithmetic and copies ran while one was open for 0% -> 0% of each run, Pallas kernels for 0% -> 6%
where the time goes in v2:
time: 55.5 us; the launch traced here: 55.1 us
  starting transfers between devices  27.8 us (50%)
  Pallas kernels  12.3 us (22%)
  waiting for transfers between devices  11.4 us (21%)
  local copies, waits for them, and re-layouts  2.83 us (5%)
  between operations  0.76 us (1%)
    ppermute x4, starting transfers between devices, shifted(): return lax.ppermute(block, axis, route)  27.8 us
    ppermute x4, waiting for transfers between devices, shifted(): return lax.ppermute(block, axis, route)  11.4 us
    pallas_call x1, Pallas kernels, body(): pl.pallas_call(late_kernel, in_specs=[vmem] * 7, out_specs=[vmem] * 3, ou...  6.72 us
    pallas_call x1, Pallas kernels, body(): pl.pallas_call(early_kernel, in_specs=[smem] * 3 + [vmem], out_specs=[vme...  3.51 us
    unnamed x14, local copies, waits for them, and re-layouts  2.81 us
    pallas_call x1, Pallas kernels, body(): pl.pallas_call(place_kernel, in_specs=[smem, vmem, vmem, vmem], out_specs...  2.06 us
  transfers between devices with their start and end apart: 4, of which 2 were waited for; matrix products, arithmetic and copies ran while one was open for 0% of the time, Pallas kernels for 6%

profile of v2, /device:TPU:8, one launch (start us, length us, event | category | flops | bytes accessed | tf_op | source)
XLA Modules:
  0.0 55.1 jit_solution(6502866199403468710)
XLA Ops:
  0.6 0.0 copy-start.3
  0.6 0.7 %copy-done.3 = s32[2,4]{1,0:T(2,128)S(1)} copy-done((s32[2,4]{1,0:T(2,128)S(1)}, s32[2,4]{1,0:T(2,128)}, u32[]{:S(2)}) %copy-start.3) | copy-done | bytes 56
  1.3 0.7 %copy-done = f32[3,2,4,128]{3,2,1,0:T(4,128)S(1)} copy-done((f32[3,2,4,128]{3,2,1,0:T(4,128)S(1)}, f32[3,2,4,128]{3,2,1,0:T(4,128)}, u32[]{:S(2)}) %copy-start) | copy-done | bytes 12312
  2.0 0.0 copy-start.1
  2.0 0.7 %copy-done.1 = f32[3,2,4,128]{3,2,1,0:T(4,128)S(1)} copy-done((f32[3,2,4,128]{3,2,1,0:T(4,128)S(1)}, f32[3,2,4,128]{3,2,1,0:T(4,128)}, u32[]{:S(2)}) %copy-start.1) | copy-done | bytes 12312
  2.7 0.0 copy-start.2
  2.7 0.7 %copy-done.2 = f32[3,2,4,128]{3,2,1,0:T(4,128)S(1)} copy-done((f32[3,2,4,128]{3,2,1,0:T(4,128)S(1)}, f32[3,2,4,128]{3,2,1,0:T(4,128)}, u32[]{:S(2)}) %copy-start.2) | copy-done | bytes 12312
  3.4 2.1 %place.1 = (f32[3,8,128]{2,1,0:T(8,128)}, f32[3,8,128]{2,1,0:T(8,128)S(1)}, f32[3,8,128]{2,1,0:T(8,128)S(1)}, s32[8,128]{1,0:T(8,128)S(1)}) custom-call(s32[2,4]{1,0:T(2,128)S(1)} %copy-done.3, f32[3,8,128]{2,1,0:T(8,128)S(1)} %bitcast.11, f32[3,8,128]{2,1,0:T(8,128)S(1)} %bitcast.12, f32[3,8,128]{2,1,0:T(8,128)S(1)} %bitcast.13), custom_call_target="tpu_custom_call" | custom-call | tf_op jit(solution)/shard_map/place/pallas_call | solution.py:321
  5.5 13.9 %collective-permute-start.1 = (f32[3,2,4,128]{3,2,1,0:T(4,128)S(1)}, f32[3,2,4,128]{3,2,1,0:T(4,128)S(1)}, u32[]{:S(2)}, u32[]{:S(2)}) collective-permute-start(f32[3,2,4,128]{3,2,1,0:T(4,128)S(1)} %bitcast.8), channel_id=1, source_target_pairs={{0,760},{8,0},{16,8},{24,16},{32,24},{40,32},{48,40},{56,48},{64,5... | collective-permute-start | bytes 36872 | tf_op jit(solution)/shard_map/ppermute | solution.py:312
  19.4 1.9 %collective-permute-start = (f32[3,2,4,128]{3,2,1,0:T(4,128)S(1)}, f32[3,2,4,128]{3,2,1,0:T(4,128)S(1)}, u32[]{:S(2)}, u32[]{:S(2)}) collective-permute-start(f32[3,2,4,128]{3,2,1,0:T(4,128)S(1)} %bitcast.9), channel_id=1, source_target_pairs={{0,8},{8,16},{16,24},{24,32},{32,40},{40,48},{48,56},{56,64},{64,7... | collective-permute-start | bytes 36872 | tf_op jit(solution)/shard_map/ppermute | solution.py:312
  21.3 0.0 collective-permute-done.1
  21.3 5.2 %collective-permute-done = f32[3,2,4,128]{3,2,1,0:T(4,128)S(1)} collective-permute-done((f32[3,2,4,128]{3,2,1,0:T(4,128)S(1)}, f32[3,2,4,128]{3,2,1,0:T(4,128)S(1)}, u32[]{:S(2)}, u32[]{:S(2)}) %collective-permute-start) | collective-permute-done | bytes 12320 | tf_op jit(solution)/shard_map/ppermute | solution.py:312
  26.6 0.0 copy-start.4
  26.6 0.0 copy-start.5
  26.6 0.0 copy-start.6
  26.6 10.1 %collective-permute-start.3 = (f32[3,6,2,128]{3,2,1,0:T(2,128)S(1)}, f32[3,6,2,128]{3,2,1,0:T(2,128)S(1)}, u32[]{:S(2)}, u32[]{:S(2)}) collective-permute-start(f32[3,6,2,128]{3,2,1,0:T(2,128)S(1)} %get-tuple-element.22), channel_id=1, source_target_pairs={{0,7},{1,0},{2,1},{3,2},{4,3},{5,4},{6,5},{7,6},{8,15},{9,8},{10,9... | collective-permute-start | bytes 55304 | tf_op jit(solution)/shard_map/ppermute | solution.py:312
  36.7 1.9 %collective-permute-start.2 = (f32[3,6,2,128]{3,2,1,0:T(2,128)S(1)}, f32[3,6,2,128]{3,2,1,0:T(2,128)S(1)}, u32[]{:S(2)}, u32[]{:S(2)}) collective-permute-start(f32[3,6,2,128]{3,2,1,0:T(2,128)S(1)} %get-tuple-element.23), channel_id=1, source_target_pairs={{0,1},{1,2},{2,3},{3,4},{4,5},{5,6},{6,7},{7,0},{8,9},{9,10},{10,1... | collective-permute-start | bytes 55304 | tf_op jit(solution)/shard_map/ppermute | solution.py:312
  38.6 0.0 copy-done.4
  38.6 0.0 copy-done.5
  38.6 0.0 copy-done.6
  38.6 3.5 %early.1 = (f32[16,128]{1,0:T(8,128)S(1)}, f32[16,128]{1,0:T(8,128)S(1)}) custom-call(f32[4]{0:T(128)S(1)} %copy-done.4, f32[4]{0:T(128)S(1)} %copy-done.5, f32[2]{0:T(128)S(1)} %copy-done.6, f32[3,6,4,128]{3,2,1,0:T(4,128)S(1)} %pad_maximum_fusion.mid_ref), custom_call_target="tpu_custom_call" | custom-call | flops 12000000 | bytes 60000 | tf_op jit(solution)/shard_map/early/pallas_call | solution.py:336
  42.1 0.0 collective-permute-done.3.high_ref
  42.2 6.2 %collective-permute-done.2.low_ref = f32[3,6,2,128]{3,2,1,0:T(2,128)S(1)} collective-permute-done((f32[3,6,2,128]{3,2,1,0:T(2,128)S(1)}, f32[3,6,2,128]{3,2,1,0:T(2,128)S(1)}, u32[]{:S(2)}, u32[]{:S(2)}) %collective-permute-start.2) | collective-permute-done | bytes 18464 | tf_op jit(solution)/shard_map/ppermute | solution.py:312
  48.3 6.7 %late.1 = (f32[3,8,128]{2,1,0:T(8,128)}, f32[3,8,128]{2,1,0:T(8,128)}, f32[6,8,128]{2,1,0:T(8,128)}) custom-call(f32[3,6,4,128]{3,2,1,0:T(4,128)S(1)} %pad_maximum_fusion.mid_ref, f32[3,6,2,128]{3,2,1,0:T(2,128)S(1)} %collective-permute-done.2.low_ref, f32[3,6,2,128]{3,2,1,0:T(2,128)S(1)} %collective-permute-done.3.high_ref, ...), custom_call_target="tpu_custom_call" | custom-call | tf_op jit(solution)/shard_map/late/pallas_call | solution.py:346
  (3 shorter events, 0.0 us)
Async XLA Ops:
  0.6 0.7 %copy-start.3 = (s32[2,4]{1,0:T(2,128)S(1)}, s32[2,4]{1,0:T(2,128)}, u32[]{:S(2)}) copy-start(s32[2,4]{1,0:T(2,128)} %counts_ref.1) | copy-start | bytes 100
  1.3 0.7 %copy-start = (f32[3,2,4,128]{3,2,1,0:T(4,128)S(1)}, f32[3,2,4,128]{3,2,1,0:T(4,128)}, u32[]{:S(2)}) copy-start(f32[3,2,4,128]{3,2,1,0:T(4,128)} %param.7) | copy-start | bytes 36868
  2.0 0.7 %copy-start.1 = (f32[3,2,4,128]{3,2,1,0:T(4,128)S(1)}, f32[3,2,4,128]{3,2,1,0:T(4,128)}, u32[]{:S(2)}) copy-start(f32[3,2,4,128]{3,2,1,0:T(4,128)} %param.8) | copy-start | bytes 36868
  2.7 0.7 %copy-start.2 = (f32[3,2,4,128]{3,2,1,0:T(4,128)S(1)}, f32[3,2,4,128]{3,2,1,0:T(4,128)}, u32[]{:S(2)}) copy-start(f32[3,2,4,128]{3,2,1,0:T(4,128)} %param.9) | copy-start | bytes 36868
  5.5 15.8 %collective-permute-start.1 = (f32[3,2,4,128]{3,2,1,0:T(4,128)S(1)}, f32[3,2,4,128]{3,2,1,0:T(4,128)S(1)}, u32[]{:S(2)}, u32[]{:S(2)}) collective-permute-start(f32[3,2,4,128]{3,2,1,0:T(4,128)S(1)} %bitcast.8), channel_id=1, source_target_pairs={{0,760},{8,0},{16,8},{24,16},{32,24},{40,32},{48,40},{56,48},{64,5... | collective-permute-start | bytes 36872 | tf_op jit(solution)/shard_map/ppermute | solution.py:312
  19.4 7.1 %collective-permute-start = (f32[3,2,4,128]{3,2,1,0:T(4,128)S(1)}, f32[3,2,4,128]{3,2,1,0:T(4,128)S(1)}, u32[]{:S(2)}, u32[]{:S(2)}) collective-permute-start(f32[3,2,4,128]{3,2,1,0:T(4,128)S(1)} %bitcast.9), channel_id=1, source_target_pairs={{0,8},{8,16},{16,24},{24,32},{32,40},{40,48},{48,56},{56,64},{64,7... | collective-permute-start | bytes 36872 | tf_op jit(solution)/shard_map/ppermute | solution.py:312
  26.6 12.0 %copy-start.4 = (f32[4]{0:T(128)S(1)}, f32[4]{0:T(128)}, u32[]{:S(2)}) copy-start(f32[4]{0:T(128)} %dens_ref.1) | copy-start | bytes 52
  26.6 12.0 %copy-start.5 = (f32[4]{0:T(128)S(1)}, f32[4]{0:T(128)}, u32[]{:S(2)}) copy-start(f32[4]{0:T(128)} %pair_ref.1) | copy-start | bytes 52
  26.6 12.0 %copy-start.6 = (f32[2]{0:T(128)S(1)}, f32[2]{0:T(128)}, u32[]{:S(2)}) copy-start(f32[2]{0:T(128)} %emb_ref.1) | copy-start | bytes 28
  26.6 15.5 %collective-permute-start.3 = (f32[3,6,2,128]{3,2,1,0:T(2,128)S(1)}, f32[3,6,2,128]{3,2,1,0:T(2,128)S(1)}, u32[]{:S(2)}, u32[]{:S(2)}) collective-permute-start(f32[3,6,2,128]{3,2,1,0:T(2,128)S(1)} %get-tuple-element.22), channel_id=1, source_target_pairs={{0,7},{1,0},{2,1},{3,2},{4,3},{5,4},{6,5},{7,6},{8,15},{9,8},{10,9... | collective-permute-start | bytes 55304 | tf_op jit(solution)/shard_map/ppermute | solution.py:312
  36.7 11.7 %collective-permute-start.2 = (f32[3,6,2,128]{3,2,1,0:T(2,128)S(1)}, f32[3,6,2,128]{3,2,1,0:T(2,128)S(1)}, u32[]{:S(2)}, u32[]{:S(2)}) collective-permute-start(f32[3,6,2,128]{3,2,1,0:T(2,128)S(1)} %get-tuple-element.23), channel_id=1, source_target_pairs={{0,1},{1,2},{2,3},{3,4},{4,5},{5,6},{6,7},{7,0},{8,9},{9,10},{10,1... | collective-permute-start | bytes 55304 | tf_op jit(solution)/shard_map/ppermute | solution.py:312

commit v3 on v2

--- a/solution.py
+++ b/solution.py
@@ -1,11 +1,10 @@
-import functools
-
 import jax
 import jax.numpy as jnp
 from jax import lax
 from jax.experimental import pallas as pl
 from jax.experimental.pallas import tpu as pltpu
 from jax.sharding import PartitionSpec as P
+
 
 cutoff = 5.5
 time_step = 0.004
@@ -21,7 +20,21 @@
 GRANT = 8 * 2**20
 
 
-def place_kernel(counts_ref, pos_ref, vel_ref, frc_ref, new_ref, half_ref, pay_ref, slot_ref):
+def place_kernel(
+    counts_hbm, pos_hbm, vel_hbm, frc_hbm,
+    new_ref, half_ref, pay_ref, slot_ref,
+    fetched, counts_ref, arrived,
+):
+    copies = [
+        pltpu.make_async_copy(source, fetched.at[k], arrived.at[k])
+        for k, source in enumerate((pos_hbm, vel_hbm, frc_hbm))
+    ]
+    copies.append(pltpu.make_async_copy(counts_hbm, counts_ref, arrived.at[3]))
+    for copy in copies:
+        copy.start()
+    for copy in copies:
+        copy.wait()
+    pos_ref, vel_ref, frc_ref = [fetched.at[k] for k in range(3)]
     half = [vel_ref[c] + kick_scale * frc_ref[c] for c in range(3)]
     new = [pos_ref[c] + time_step * half[c] for c in range(3)]
     for c in range(3):
@@ -107,10 +120,17 @@
     return lax.fori_loop(0, jnp.minimum(reach + 1, SLOTS // 2), pair, start)
 
 
-def density_term(square, a):
+def monic(coefs):
+    return [c / coefs[3] for c in coefs[:3]]
+
+
+def cubic(w, m):
+    return m[0] + w * (m[1] + w * (m[2] + w))
+
+
+def density_term(square, m):
     w = jnp.maximum(1.0 - square, 0.0)
-    value = a[0] + w * (a[1] + w * (a[2] + w * a[3]))
-    return (w * w) * value
+    return (w * w) * cubic(w, m)
 
 
 def square_of(mine, others):
@@ -138,7 +158,7 @@
                 source[base + low : base + high] = block
                 for edge in (0,) * low + (3,) * (4 - high):
                     source[base + edge : base + edge + 1] = jnp.full((1, SLOTS), FAR, jnp.float32)
-    a = [dens_ref[k] for k in range(4)]
+    a = monic([jnp.full((8, SLOTS), dens_ref[k], jnp.float32) for k in range(4)])
 
     def rows_of(ref, u, v, c, m):
         start = 24 * (3 * (v + 1) + c) + 4 * (1 + u) + 8 * m
@@ -198,6 +218,7 @@
 
     a = [coef(k) for k in range(4)]
     p = [coef(4 + k) for k in range(4)]
+    am = monic(a)
 
     def rim(ref, u, v, c):
         start = 12 * (3 * (v + 1) + c) + 2 * (1 + u)
@@ -219,9 +240,9 @@
                 square = square_of(outer, others)
                 if u == 0 and v == 0:
                     square = square + same
-                out = out + density_term(square, a)
+                out = out + density_term(square, am)
                 if v == 0:
-                    inn = inn + density_term(square_of(inner, others), a)
+                    inn = inn + density_term(square_of(inner, others), am)
         return (out, inn)
 
     zero = jnp.zeros((8, SLOTS), f32)
@@ -238,10 +259,9 @@
             )
         slopes[6 * x + 2 : 6 * x + 4] = sum_ref[4 * x + 1 : 4 * x + 3]
     for m in range(3):
-        total = slopes[8 * m : 8 * m + 8]
-        slopes[8 * m : 8 * m + 8] = (-0.5 * coef(8)) / jnp.sqrt(1.0 + total) + (
-            2.0 * coef(9)
-        ) * total
+        total = slopes[8 * m : 8 * m + 8] * a[3]
+        slope = (-0.5 * coef(8)) / jnp.sqrt(1.0 + total) + (2.0 * coef(9)) * total
+        slopes[8 * m : 8 * m + 8] = slope * (a[3] / p[3])
 
     for u in (-1, 0, 1):
         for v in (-1, 0, 1):
@@ -267,8 +287,8 @@
         return ref[8 * (4 * k + c) : 8 * (4 * k + c) + 8]
 
     own = [member(packs, 4, c) for c in range(4)]
-    gd = [(k + 2.0) * a[k] for k in range(4)]
-    gp = [(k + 2.0) * p[k] for k in range(4)]
+    gd = monic([(k + 2.0) * a[k] for k in range(4)])
+    gp = monic([(k + 2.0) * p[k] for k in range(4)])
 
     def force_step(d, ref, sums):
         same = jnp.where(d == 0, 100.0, 0.0)
@@ -280,9 +300,7 @@
                 square = square + same
             w = jnp.maximum(1.0 - square, 0.0)
             slope = own[3] + member(ref, k, 3)
-            dens = gd[0] + w * (gd[1] + w * (gd[2] + w * gd[3]))
-            pair = gp[0] + w * (gp[1] + w * (gp[2] + w * gp[3]))
-            strength = w * (slope * dens + pair)
+            strength = w * (slope * cubic(w, gd) + cubic(w, gp))
             pulls = [strength * gap for gap in gaps]
             for c in range(3):
                 sums[c] = sums[c] + pulls[c]
@@ -296,14 +314,15 @@
     index = jnp.maximum(slot, 0)
 
     def restored(values, scale):
-        return jnp.where(alive, jnp.take_along_axis(values, index, axis=1) * scale, 0.0)
+        moved = jnp.take_along_axis(values, index, axis=1)
+        return jnp.where(alive, moved * (scale * p[3]), 0.0)
 
     for c in range(3):
-        force = restored(sums[c], 2.0 / cutoff)
+        force = restored(sums[c], 10.0 / cutoff)
         frc_ref[c] = force
         vel_ref[c] = half_ref[c] + kick_scale * force
     for t in range(6):
-        str_ref[t] = restored(sums[3 + t], 1.0 / atom_volume)
+        str_ref[t] = restored(sums[3 + t], 5.0 / atom_volume)
 
 
 def shifted(block, axis, distance):
@@ -317,19 +336,35 @@
     flat = (3, 8, SLOTS)
     vmem = pl.BlockSpec(memory_space=pltpu.VMEM)
     smem = pl.BlockSpec(memory_space=pltpu.SMEM)
+    hbm = pl.BlockSpec(memory_space=pltpu.HBM)
     f32 = jnp.float32
     new, half, pay, slot = pl.pallas_call(
         place_kernel,
-        in_specs=[smem, vmem, vmem, vmem],
+        in_specs=[hbm] * 4,
         out_specs=[vmem] * 4,
         out_shape=[jax.ShapeDtypeStruct(flat, f32)] * 3
         + [jax.ShapeDtypeStruct((8, SLOTS), jnp.int32)],
+        scratch_shapes=[
+            pltpu.VMEM((3,) + flat, f32),
+            pltpu.SMEM(counts.shape, jnp.int32),
+            pltpu.SemaphoreType.DMA((4,)),
+        ],
         compiler_params=pltpu.CompilerParams(vmem_limit_bytes=GRANT),
         name="place",
-    )(counts, position.reshape(flat), velocity.reshape(flat), force_old.reshape(flat))
+    )(
+        *[
+            pltpu.with_memory_space_constraint(source, pltpu.HBM)
+            for source in (
+                counts,
+                position.reshape(flat),
+                velocity.reshape(flat),
+                force_old.reshape(flat),
+            )
+        ],
+    )
     pay = pay.reshape(shape)
+    before = shifted(pay, "gx", 1)
     after = shifted(pay, "gx", -1)
-    before = shifted(pay, "gx", 1)
     mid = jnp.concatenate([before, pay, after], axis=1)
     high = shifted(mid[:, :, :2], "gy", -1)
     low = shifted(mid[:, :, 2:], "gy", 1)

time: 55.5 us -> 52.7 us (0.950)
  local copies, waits for them, and re-layouts: 2.83 us -> 0.04 us
    unnamed x14 -> x6, local copies, waits for them, and re-layouts: 2.81 us -> 0.02 us
where the time goes in v3:
time: 52.7 us; the launch traced here: 52.4 us
  starting transfers between devices  27.8 us (53%)
  Pallas kernels  12.3 us (23%)
  waiting for transfers between devices  11.5 us (22%)
  between operations  0.75 us (1%)
    ppermute x4, starting transfers between devices, shifted(): return lax.ppermute(block, axis, route)  27.8 us
    ppermute x4, waiting for transfers between devices, shifted(): return lax.ppermute(block, axis, route)  11.5 us
    pallas_call x1, Pallas kernels, body(): pl.pallas_call(late_kernel, in_specs=[vmem] * 7, out_specs=[vmem] * 3, ou...  6.56 us
    pallas_call x1, Pallas kernels, body(): pl.pallas_call(early_kernel, in_specs=[smem] * 3 + [vmem], out_specs=[vme...  3.36 us
    pallas_call x1, Pallas kernels, body(): pl.pallas_call(place_kernel, in_specs=[hbm] * 4, out_specs=[vmem] * 4, ou...  2.37 us
  transfers between devices with their start and end apart: 4, of which 2 were waited for; matrix products, arithmetic and copies ran while one was open for 0% of the time, Pallas kernels for 6%

profile of v3, /device:TPU:8, one launch (start us, length us, event | category | flops | bytes accessed | tf_op | source)
XLA Modules:
  0.0 52.4 jit_solution(12101368137692953881)
XLA Ops:
  0.6 2.4 %place.1 = (f32[3,8,128]{2,1,0:T(8,128)}, f32[3,8,128]{2,1,0:T(8,128)S(1)}, f32[3,8,128]{2,1,0:T(8,128)S(1)}, s32[8,128]{1,0:T(8,128)S(1)}) custom-call(s32[2,4]{1,0:T(2,128)} %counts_hbm.1, f32[3,8,128]{2,1,0:T(8,128)} %bitcast.11, f32[3,8,128]{2,1,0:T(8,128)} %bitcast.12, f32[3,8,128]{2,1,0:T(8,128)} %bitcast.13), custom_call_target="tpu_custom_call" | custom-call | tf_op jit(solution)/shard_map/place/pallas_call | solution.py:341
  3.0 13.9 %collective-permute-start.1 = (f32[3,2,4,128]{3,2,1,0:T(4,128)S(1)}, f32[3,2,4,128]{3,2,1,0:T(4,128)S(1)}, u32[]{:S(2)}, u32[]{:S(2)}) collective-permute-start(f32[3,2,4,128]{3,2,1,0:T(4,128)S(1)} %bitcast.8), channel_id=1, source_target_pairs={{0,760},{8,0},{16,8},{24,16},{32,24},{40,32},{48,40},{56,48},{64,5... | collective-permute-start | bytes 36872 | tf_op jit(solution)/shard_map/ppermute | solution.py:331
  16.9 1.9 %collective-permute-start = (f32[3,2,4,128]{3,2,1,0:T(4,128)S(1)}, f32[3,2,4,128]{3,2,1,0:T(4,128)S(1)}, u32[]{:S(2)}, u32[]{:S(2)}) collective-permute-start(f32[3,2,4,128]{3,2,1,0:T(4,128)S(1)} %bitcast.9), channel_id=1, source_target_pairs={{0,8},{8,16},{16,24},{24,32},{32,40},{40,48},{48,56},{56,64},{64,7... | collective-permute-start | bytes 36872 | tf_op jit(solution)/shard_map/ppermute | solution.py:331
  18.9 0.0 collective-permute-done.1
  18.9 5.2 %collective-permute-done = f32[3,2,4,128]{3,2,1,0:T(4,128)S(1)} collective-permute-done((f32[3,2,4,128]{3,2,1,0:T(4,128)S(1)}, f32[3,2,4,128]{3,2,1,0:T(4,128)S(1)}, u32[]{:S(2)}, u32[]{:S(2)}) %collective-permute-start) | collective-permute-done | bytes 12320 | tf_op jit(solution)/shard_map/ppermute | solution.py:331
  24.1 0.0 copy-start
  24.1 0.0 copy-start.1
  24.1 0.0 copy-start.2
  24.1 10.1 %collective-permute-start.3 = (f32[3,6,2,128]{3,2,1,0:T(2,128)S(1)}, f32[3,6,2,128]{3,2,1,0:T(2,128)S(1)}, u32[]{:S(2)}, u32[]{:S(2)}) collective-permute-start(f32[3,6,2,128]{3,2,1,0:T(2,128)S(1)} %get-tuple-element.22), channel_id=1, source_target_pairs={{0,7},{1,0},{2,1},{3,2},{4,3},{5,4},{6,5},{7,6},{8,15},{9,8},{10,9... | collective-permute-start | bytes 55304 | tf_op jit(solution)/shard_map/ppermute | solution.py:331
  34.2 1.9 %collective-permute-start.2 = (f32[3,6,2,128]{3,2,1,0:T(2,128)S(1)}, f32[3,6,2,128]{3,2,1,0:T(2,128)S(1)}, u32[]{:S(2)}, u32[]{:S(2)}) collective-permute-start(f32[3,6,2,128]{3,2,1,0:T(2,128)S(1)} %get-tuple-element.23), channel_id=1, source_target_pairs={{0,1},{1,2},{2,3},{3,4},{4,5},{5,6},{6,7},{7,0},{8,9},{9,10},{10,1... | collective-permute-start | bytes 55304 | tf_op jit(solution)/shard_map/ppermute | solution.py:331
  36.1 0.0 copy-done
  36.1 0.0 copy-done.1
  36.1 0.0 copy-done.2
  36.1 3.4 %early.1 = (f32[16,128]{1,0:T(8,128)S(1)}, f32[16,128]{1,0:T(8,128)S(1)}) custom-call(f32[4]{0:T(128)S(1)} %copy-done, f32[4]{0:T(128)S(1)} %copy-done.1, f32[2]{0:T(128)S(1)} %copy-done.2, f32[3,6,4,128]{3,2,1,0:T(4,128)S(1)} %pad_maximum_fusion.mid_ref), custom_call_target="tpu_custom_call" | custom-call | flops 12000000 | bytes 60000 | tf_op jit(solution)/shard_map/early/pallas_call | solution.py:371
  39.5 0.0 collective-permute-done.3.high_ref
  39.5 6.3 %collective-permute-done.2.low_ref = f32[3,6,2,128]{3,2,1,0:T(2,128)S(1)} collective-permute-done((f32[3,6,2,128]{3,2,1,0:T(2,128)S(1)}, f32[3,6,2,128]{3,2,1,0:T(2,128)S(1)}, u32[]{:S(2)}, u32[]{:S(2)}) %collective-permute-start.2) | collective-permute-done | bytes 18464 | tf_op jit(solution)/shard_map/ppermute | solution.py:331
  45.9 6.6 %late.1 = (f32[3,8,128]{2,1,0:T(8,128)}, f32[3,8,128]{2,1,0:T(8,128)}, f32[6,8,128]{2,1,0:T(8,128)}) custom-call(f32[3,6,4,128]{3,2,1,0:T(4,128)S(1)} %pad_maximum_fusion.mid_ref, f32[3,6,2,128]{3,2,1,0:T(2,128)S(1)} %collective-permute-done.2.low_ref, f32[3,6,2,128]{3,2,1,0:T(2,128)S(1)} %collective-permute-done.3.high_ref, ...), custom_call_target="tpu_custom_call" | custom-call | tf_op jit(solution)/shard_map/late/pallas_call | solution.py:381
  (2 shorter events, 0.0 us)
Async XLA Ops:
  3.0 15.9 %collective-permute-start.1 = (f32[3,2,4,128]{3,2,1,0:T(4,128)S(1)}, f32[3,2,4,128]{3,2,1,0:T(4,128)S(1)}, u32[]{:S(2)}, u32[]{:S(2)}) collective-permute-start(f32[3,2,4,128]{3,2,1,0:T(4,128)S(1)} %bitcast.8), channel_id=1, source_target_pairs={{0,760},{8,0},{16,8},{24,16},{32,24},{40,32},{48,40},{56,48},{64,5... | collective-permute-start | bytes 36872 | tf_op jit(solution)/shard_map/ppermute | solution.py:331
  16.9 7.1 %collective-permute-start = (f32[3,2,4,128]{3,2,1,0:T(4,128)S(1)}, f32[3,2,4,128]{3,2,1,0:T(4,128)S(1)}, u32[]{:S(2)}, u32[]{:S(2)}) collective-permute-start(f32[3,2,4,128]{3,2,1,0:T(4,128)S(1)} %bitcast.9), channel_id=1, source_target_pairs={{0,8},{8,16},{16,24},{24,32},{32,40},{40,48},{48,56},{56,64},{64,7... | collective-permute-start | bytes 36872 | tf_op jit(solution)/shard_map/ppermute | solution.py:331
  24.1 12.0 %copy-start = (f32[4]{0:T(128)S(1)}, f32[4]{0:T(128)}, u32[]{:S(2)}) copy-start(f32[4]{0:T(128)} %dens_ref.1) | copy-start | bytes 52
  24.1 12.0 %copy-start.1 = (f32[4]{0:T(128)S(1)}, f32[4]{0:T(128)}, u32[]{:S(2)}) copy-start(f32[4]{0:T(128)} %pair_ref.1) | copy-start | bytes 52
  24.1 12.0 %copy-start.2 = (f32[2]{0:T(128)S(1)}, f32[2]{0:T(128)}, u32[]{:S(2)}) copy-start(f32[2]{0:T(128)} %emb_ref.1) | copy-start | bytes 28
  24.1 15.4 %collective-permute-start.3 = (f32[3,6,2,128]{3,2,1,0:T(2,128)S(1)}, f32[3,6,2,128]{3,2,1,0:T(2,128)S(1)}, u32[]{:S(2)}, u32[]{:S(2)}) collective-permute-start(f32[3,6,2,128]{3,2,1,0:T(2,128)S(1)} %get-tuple-element.22), channel_id=1, source_target_pairs={{0,7},{1,0},{2,1},{3,2},{4,3},{5,4},{6,5},{7,6},{8,15},{9,8},{10,9... | collective-permute-start | bytes 55304 | tf_op jit(solution)/shard_map/ppermute | solution.py:331
  34.2 11.7 %collective-permute-start.2 = (f32[3,6,2,128]{3,2,1,0:T(2,128)S(1)}, f32[3,6,2,128]{3,2,1,0:T(2,128)S(1)}, u32[]{:S(2)}, u32[]{:S(2)}) collective-permute-start(f32[3,6,2,128]{3,2,1,0:T(2,128)S(1)} %get-tuple-element.23), channel_id=1, source_target_pairs={{0,1},{1,2},{2,3},{3,4},{4,5},{5,6},{6,7},{7,0},{8,9},{9,10},{10,1... | collective-permute-start | bytes 55304 | tf_op jit(solution)/shard_map/ppermute | solution.py:331

commit v4 on v3

--- a/solution.py
+++ b/solution.py
@@ -366,9 +366,11 @@
     before = shifted(pay, "gx", 1)
     after = shifted(pay, "gx", -1)
     mid = jnp.concatenate([before, pay, after], axis=1)
-    high = shifted(mid[:, :, :2], "gy", -1)
-    low = shifted(mid[:, :, 2:], "gy", 1)
-    total, coefs = pl.pallas_call(
+    count = lax.axis_size("gy")
+    even = lax.axis_index("gy") % 2 == 0
+    swap = [(i, i + 1 - 2 * (i % 2)) for i in range(count)]
+    mate = lax.ppermute(mid, "gy", swap)
+    early = pl.pallas_call(
         early_kernel,
         in_specs=[smem] * 3 + [vmem],
         out_specs=[vmem] * 2,
@@ -377,7 +379,13 @@
         cost_estimate=pl.CostEstimate(flops=12000000, bytes_accessed=60000, transcendentals=0),
         compiler_params=pltpu.CompilerParams(vmem_limit_bytes=GRANT),
         name="early",
-    )(density_coef, pair_coef, embed_coef, mid)
+    )
+    total, coefs = early(density_coef, pair_coef, embed_coef, mid)
+    passed = jnp.where(even, mate[:, :, 2:], mate[:, :, :2])
+    route = [(i, (i + 2 - 4 * (i % 2)) % count) for i in range(count)]
+    far = lax.ppermute(passed, "gy", route)
+    low = jnp.where(even, far, mate[:, :, 2:])
+    high = jnp.where(even, mate[:, :, :2], far)
     vel, frc, stress = pl.pallas_call(
         late_kernel,
         in_specs=[vmem] * 7,

time: 52.7 us -> 52.6 us (level)
  the two profiles are of different devices: /device:TPU:8 before, /device:TPU:2 now
where the time goes in v4:
time: 52.6 us; the launch traced here: 52.4 us
  starting transfers between devices  27.4 us (52%)
  Pallas kernels  12.4 us (24%)
  waiting for transfers between devices  11.7 us (22%)
  between operations  0.77 us (1%)
    ppermute x2, starting transfers between devices, shifted(): return lax.ppermute(block, axis, route)  19 us
    ppermute x2, waiting for transfers between devices, shifted(): return lax.ppermute(block, axis, route)  6.99 us
    pallas_call x1, Pallas kernels, body(): pl.pallas_call(late_kernel, in_specs=[vmem] * 7, out_specs=[vmem] * 3, ou...  6.56 us
    ppermute x1, starting transfers between devices, body(): mate = lax.ppermute(mid, 'gy', swap)  5.04 us
    ppermute x1, waiting for transfers between devices, body(): mate = lax.ppermute(mid, 'gy', swap)  4.7 us
    pallas_call x1, Pallas kernels, body(): total, coefs = early(density_coef, pair_coef, embed_coef, mid)  3.5 us
    ppermute x1, starting transfers between devices, body(): far = lax.ppermute(passed, 'gy', route)  3.4 us
    pallas_call x1, Pallas kernels, body(): pl.pallas_call(place_kernel, in_specs=[hbm] * 4, out_specs=[vmem] * 4, ou...  2.37 us
  transfers between devices with their start and end apart: 4, of which 2 were waited for; matrix products, arithmetic and copies ran while one was open for 0% of the time, Pallas kernels for 7%

profile of v4, /device:TPU:2, one launch (start us, length us, event | category | flops | bytes accessed | tf_op | source)
XLA Modules:
  0.0 52.4 jit_solution(2921767633973443126)
XLA Ops:
  0.6 2.4 %place.1 = (f32[3,8,128]{2,1,0:T(8,128)}, f32[3,8,128]{2,1,0:T(8,128)S(1)}, f32[3,8,128]{2,1,0:T(8,128)S(1)}, s32[8,128]{1,0:T(8,128)S(1)}) custom-call(s32[2,4]{1,0:T(2,128)} %counts_hbm.1, f32[3,8,128]{2,1,0:T(8,128)} %bitcast.11, f32[3,8,128]{2,1,0:T(8,128)} %bitcast.12, f32[3,8,128]{2,1,0:T(8,128)} %bitcast.13), custom_call_target="tpu_custom_call" | custom-call | tf_op jit(solution)/shard_map/place/pallas_call | solution.py:341
  3.0 17.1 %collective-permute-start.1 = (f32[3,2,4,128]{3,2,1,0:T(4,128)S(1)}, f32[3,2,4,128]{3,2,1,0:T(4,128)S(1)}, u32[]{:S(2)}, u32[]{:S(2)}) collective-permute-start(f32[3,2,4,128]{3,2,1,0:T(4,128)S(1)} %bitcast.8), channel_id=1, source_target_pairs={{0,760},{8,0},{16,8},{24,16},{32,24},{40,32},{48,40},{56,48},{64,5... | collective-permute-start | bytes 36872 | tf_op jit(solution)/shard_map/ppermute | solution.py:331
  20.1 1.9 %collective-permute-start = (f32[3,2,4,128]{3,2,1,0:T(4,128)S(1)}, f32[3,2,4,128]{3,2,1,0:T(4,128)S(1)}, u32[]{:S(2)}, u32[]{:S(2)}) collective-permute-start(f32[3,2,4,128]{3,2,1,0:T(4,128)S(1)} %bitcast.9), channel_id=1, source_target_pairs={{0,8},{8,16},{16,24},{24,32},{32,40},{40,48},{48,56},{56,64},{64,7... | collective-permute-start | bytes 36872 | tf_op jit(solution)/shard_map/ppermute | solution.py:331
  22.0 0.0 collective-permute-done.1
  22.0 7.0 %collective-permute-done = f32[3,2,4,128]{3,2,1,0:T(4,128)S(1)} collective-permute-done((f32[3,2,4,128]{3,2,1,0:T(4,128)S(1)}, f32[3,2,4,128]{3,2,1,0:T(4,128)S(1)}, u32[]{:S(2)}, u32[]{:S(2)}) %collective-permute-start) | collective-permute-done | bytes 12320 | tf_op jit(solution)/shard_map/ppermute | solution.py:331
  29.0 5.0 %collective-permute-start.2 = (f32[3,6,4,128]{3,2,1,0:T(4,128)S(1)}, f32[3,6,4,128]{3,2,1,0:T(4,128)S(1)}, u32[]{:S(2)}, u32[]{:S(2)}) collective-permute-start(f32[3,6,4,128]{3,2,1,0:T(4,128)S(1)} %pad_maximum_fusion.mid_ref), channel_id=1, source_target_pairs={{0,1},{1,0},{2,3},{3,2},{4,5},{5,4},{6,7},{7,6},{8,9},{9,8},{10,11... | collective-permute-start | bytes 110600 | tf_op jit(solution)/shard_map/ppermute | solution.py:372
  34.1 0.0 copy-start
  34.1 0.0 copy-start.1
  34.1 0.0 copy-start.2
  34.1 4.7 %collective-permute-done.2 = f32[3,6,4,128]{3,2,1,0:T(4,128)S(1)} collective-permute-done((f32[3,6,4,128]{3,2,1,0:T(4,128)S(1)}, f32[3,6,4,128]{3,2,1,0:T(4,128)S(1)}, u32[]{:S(2)}, u32[]{:S(2)}) %collective-permute-start.2) | collective-permute-done | bytes 36896 | tf_op jit(solution)/shard_map/ppermute | solution.py:372
  38.8 3.4 %collective-permute-start.3 = (f32[3,6,2,128]{3,2,1,0:T(2,128)S(1)}, f32[3,6,2,128]{3,2,1,0:T(2,128)S(1)}, u32[]{:S(2)}, u32[]{:S(2)}) collective-permute-start(f32[3,6,2,128]{3,2,1,0:T(2,128)S(1)} %broadcast_select_fusion.2), channel_id=1, source_target_pairs={{0,2},{1,7},{2,4},{3,1},{4,6},{5,3},{6,0},{7,5},{8,10},{9,15},{10,... | collective-permute-start | bytes 55304 | tf_op jit(solution)/shard_map/ppermute | solution.py:386
  42.2 0.0 copy-done
  42.2 0.0 copy-done.1
  42.3 0.0 copy-done.2
  42.3 3.5 %early.1 = (f32[16,128]{1,0:T(8,128)S(1)}, f32[16,128]{1,0:T(8,128)S(1)}) custom-call(f32[4]{0:T(128)S(1)} %copy-done, f32[4]{0:T(128)S(1)} %copy-done.1, f32[2]{0:T(128)S(1)} %copy-done.2, f32[3,6,4,128]{3,2,1,0:T(4,128)S(1)} %pad_maximum_fusion.mid_ref), custom_call_target="tpu_custom_call" | custom-call | flops 12000000 | bytes 60000 | tf_op jit(solution)/shard_map/early/pallas_call | solution.py:383
  45.8 0.0 collective-permute-done.3
  45.8 6.6 %late.1 = (f32[3,8,128]{2,1,0:T(8,128)}, f32[3,8,128]{2,1,0:T(8,128)}, f32[6,8,128]{2,1,0:T(8,128)}) custom-call(f32[3,6,4,128]{3,2,1,0:T(4,128)S(1)} %pad_maximum_fusion.mid_ref, f32[3,6,2,128]{3,2,1,0:T(2,128)S(1)} %get-tuple-element.23.low_ref, f32[3,6,2,128]{3,2,1,0:T(2,128)S(1)} %get-tuple-element.22.high_ref, ...), custom_call_target="tpu_custom_call" | custom-call | tf_op jit(solution)/shard_map/late/pallas_call | solution.py:389
  (3 shorter events, 0.0 us)
Async XLA Ops:
  3.0 19.0 %collective-permute-start.1 = (f32[3,2,4,128]{3,2,1,0:T(4,128)S(1)}, f32[3,2,4,128]{3,2,1,0:T(4,128)S(1)}, u32[]{:S(2)}, u32[]{:S(2)}) collective-permute-start(f32[3,2,4,128]{3,2,1,0:T(4,128)S(1)} %bitcast.8), channel_id=1, source_target_pairs={{0,760},{8,0},{16,8},{24,16},{32,24},{40,32},{48,40},{56,48},{64,5... | collective-permute-start | bytes 36872 | tf_op jit(solution)/shard_map/ppermute | solution.py:331
  20.1 8.9 %collective-permute-start = (f32[3,2,4,128]{3,2,1,0:T(4,128)S(1)}, f32[3,2,4,128]{3,2,1,0:T(4,128)S(1)}, u32[]{:S(2)}, u32[]{:S(2)}) collective-permute-start(f32[3,2,4,128]{3,2,1,0:T(4,128)S(1)} %bitcast.9), channel_id=1, source_target_pairs={{0,8},{8,16},{16,24},{24,32},{32,40},{40,48},{48,56},{56,64},{64,7... | collective-permute-start | bytes 36872 | tf_op jit(solution)/shard_map/ppermute | solution.py:331
  29.0 9.8 %collective-permute-start.2 = (f32[3,6,4,128]{3,2,1,0:T(4,128)S(1)}, f32[3,6,4,128]{3,2,1,0:T(4,128)S(1)}, u32[]{:S(2)}, u32[]{:S(2)}) collective-permute-start(f32[3,6,4,128]{3,2,1,0:T(4,128)S(1)} %pad_maximum_fusion.mid_ref), channel_id=1, source_target_pairs={{0,1},{1,0},{2,3},{3,2},{4,5},{5,4},{6,7},{7,6},{8,9},{9,8},{10,11... | collective-permute-start | bytes 110600 | tf_op jit(solution)/shard_map/ppermute | solution.py:372
  34.1 8.2 %copy-start = (f32[4]{0:T(128)S(1)}, f32[4]{0:T(128)}, u32[]{:S(2)}) copy-start(f32[4]{0:T(128)} %dens_ref.1) | copy-start | bytes 52
  34.1 8.2 %copy-start.1 = (f32[4]{0:T(128)S(1)}, f32[4]{0:T(128)}, u32[]{:S(2)}) copy-start(f32[4]{0:T(128)} %pair_ref.1) | copy-start | bytes 52
  34.1 8.2 %copy-start.2 = (f32[2]{0:T(128)S(1)}, f32[2]{0:T(128)}, u32[]{:S(2)}) copy-start(f32[2]{0:T(128)} %emb_ref.1) | copy-start | bytes 28
  38.8 6.9 %collective-permute-start.3 = (f32[3,6,2,128]{3,2,1,0:T(2,128)S(1)}, f32[3,6,2,128]{3,2,1,0:T(2,128)S(1)}, u32[]{:S(2)}, u32[]{:S(2)}) collective-permute-start(f32[3,6,2,128]{3,2,1,0:T(2,128)S(1)} %broadcast_select_fusion.2), channel_id=1, source_target_pairs={{0,2},{1,7},{2,4},{3,1},{4,6},{5,3},{6,0},{7,5},{8,10},{9,15},{10,... | collective-permute-start | bytes 55304 | tf_op jit(solution)/shard_map/ppermute | solution.py:386

commit v5 on v4

--- a/solution.py
+++ b/solution.py
@@ -18,6 +18,7 @@
 FAR = 1.0e4
 NONE = -1.0e6
 GRANT = 8 * 2**20
+UNROLL = 8
 
 
 def place_kernel(
@@ -87,18 +88,26 @@
         pay_ref[c] = jnp.where(taken, moved, FAR if c == 0 else 0.0)
 
 
-def reach_of(boxes):
+def gap_range(boxes):
     most, least = (None, None)
     for far, height in boxes:
         lane = lax.broadcasted_iota(jnp.int32, height.shape, 1).astype(jnp.float32)
         gap = lane - height * (cutoff * SLOTS_PER_A)
         there = far < 100.0
-        high = jnp.max(jnp.where(there, gap, -1.0e6))
-        low = jnp.min(jnp.where(there, gap, 1.0e6))
+        high = jnp.where(there, gap, -1.0e6)
+        low = jnp.where(there, gap, 1.0e6)
         most = high if most is None else jnp.maximum(most, high)
         least = low if least is None else jnp.minimum(least, low)
-    reach = most - least + (cutoff * SLOTS_PER_A + 0.01)
+    return jnp.max(most, axis=0, keepdims=True), jnp.min(least, axis=0, keepdims=True)
+
+
+def reach_of(most, least):
+    reach = jnp.max(most) - jnp.min(least) + (cutoff * SLOTS_PER_A + 0.01)
     return jnp.clip(reach, 0.0, 64.0).astype(jnp.int32)
+
+
+def joined(one, two):
+    return jnp.maximum(one[0], two[0]), jnp.minimum(one[1], two[1])
 
 
 def offsets_loop(reach, source, turned, step, start):
@@ -109,15 +118,16 @@
         for r in range(0, rows, 8):
             ref[r : r + 8] = pltpu.roll(source[r : r + 8], by, 1)
 
-    def pair(i, carry):
-        d = 2 * i - reach
-        turn(d + 1, turned.at[1])
-        carry = step(d, turned.at[0], carry)
-        turn(d + 2, turned.at[0])
-        return step(d + 1, turned.at[1], carry)
+    def several(i, carry):
+        for k in range(UNROLL):
+            d = UNROLL * i + k - reach
+            turn(d + 1, turned.at[1 - k % 2])
+            carry = step(d, turned.at[k % 2], carry)
+        return carry
 
     turn(-reach, turned.at[0])
-    return lax.fori_loop(0, jnp.minimum(reach + 1, SLOTS // 2), pair, start)
+    trips = (2 * reach + UNROLL) // UNROLL
+    return lax.fori_loop(0, jnp.minimum(trips, SLOTS // UNROLL), several, start)
 
 
 def monic(coefs):
@@ -138,7 +148,9 @@
     return gaps[0] * gaps[0] + gaps[1] * gaps[1] + gaps[2] * gaps[2]
 
 
-def early_kernel(dens_ref, pair_ref, emb_ref, mid_ref, sum_ref, coef_ref, source, turned):
+def early_kernel(
+    dens_ref, pair_ref, emb_ref, mid_ref, sum_ref, coef_ref, range_ref, source, turned
+):
     for k in range(4):
         coef_ref[k : k + 1] = jnp.full((1, SLOTS), dens_ref[k], jnp.float32)
         coef_ref[4 + k : 5 + k] = jnp.full((1, SLOTS), pair_ref[k], jnp.float32)
@@ -179,39 +191,94 @@
         return tuple(totals)
 
     zero = jnp.zeros((8, SLOTS), jnp.float32)
-    totals = offsets_loop(reach_of(boxes), source, turned, step, (zero, zero))
+    extent = gap_range(boxes)
+    for k in range(2):
+        range_ref[k : k + 1] = extent[k]
+    totals = offsets_loop(reach_of(*extent), source, turned, step, (zero, zero))
     for m in range(2):
         sum_ref[8 * m : 8 * m + 8] = totals[m]
 
 
+def rim_density(high, mid_ref, halo_ref, rows, a, extent, source, turned, sides, out_ref):
+    sign = (2 * high - 1).astype(jnp.float32)
+
+    def depth_row(c, x, t):
+        if t == 0:
+            values = mid_ref[c, x, pl.ds(3 * high, 1)]
+        else:
+            values = halo_ref[c, x, pl.ds(rows[t - 1], 1)]
+        if c == 1:
+            return values + sign * (1.5 + t)
+        return values + (x - 2.5) if c == 0 else values
+
+    for c in range(3):
+        for x in range(6):
+            base = 24 * c + 2 * x
+            source[base : base + 1] = depth_row(c, x, 0)
+            source[base + 1 : base + 2] = depth_row(c, x, 2)
+            near = depth_row(c, x, 1)
+            source[base + 12 : base + 13] = near
+            source[base + 13 : base + 14] = near
+            if 1 <= x <= 4:
+                row = 2 * (x - 1)
+                sides[0, c, row : row + 1] = near
+                sides[0, c, row + 1 : row + 2] = near
+                sides[1, c, row : row + 1] = near
+                sides[1, c, row + 1 : row + 2] = depth_row(c, x, 0)
+    mine = [[sides[k, c] for c in range(3)] for k in range(2)]
+    row_at = lax.broadcasted_iota(jnp.int32, (8, SLOTS), 0)
+    itself = jnp.where(lax.bitwise_and(row_at, 1) == 0, 100.0, 0.0)
+
+    def step(d, ref, totals):
+        same = jnp.where(d == 0, 1.0, 0.0)
+        totals = list(totals)
+        for u in (-1, 0, 1):
+            for k in range(2):
+                starts = [24 * c + 12 * k + 2 * (1 + u) for c in range(3)]
+                square = square_of(mine[k], [ref[r : r + 8] for r in starts])
+                if u == 0 and k == 1:
+                    square = square + itself * same
+                totals[k] = totals[k] + density_term(square, a)
+        return tuple(totals)
+
+    zero = jnp.zeros((8, SLOTS), jnp.float32)
+    totals = offsets_loop(reach_of(*extent), source, turned, step, (zero, zero))
+    for k in range(2):
+        sides[k, 0] = totals[k]
+    for x in range(4):
+        row = 2 * x
+        out_ref[x : x + 1] = (
+            sides[0, 0, row : row + 1] + sides[0, 0, row + 1 : row + 2] + sides[1, 0, row : row + 1]
+        )
+        out_ref[4 + x : 5 + x] = sides[1, 0, row + 1 : row + 2]
+
+
+def side_of_mate():
+    return 1 - lax.rem(lax.axis_index("gy"), 2)
+
+
+def mate_kernel(mid_ref, mate_ref, coef_ref, range_ref, sum_ref, wide_ref, source, turned, sides):
+    high = side_of_mate()
+    boxes = [
+        (mate_ref[0, x, pl.ds(2 - 2 * high, 2)], mate_ref[2, x, pl.ds(2 - 2 * high, 2)])
+        for x in range(6)
+    ]
+    extent = joined(gap_range(boxes), (range_ref[0:1], range_ref[1:2]))
+    for k in range(2):
+        wide_ref[k : k + 1] = extent[k]
+    a = monic([jnp.broadcast_to(coef_ref[k : k + 1], (8, SLOTS)) for k in range(4)])
+    rows = (3 - 3 * high, 2 - high)
+    rim_density(high, mid_ref, mate_ref, rows, a, extent, source, turned, sides, sum_ref)
+
+
 def late_kernel(
-    mid_ref, low_ref, high_ref, half_ref, slot_ref, sum_ref, coef_ref,
+    mid_ref, mate_ref, far_ref, half_ref, slot_ref, sum_ref, rim_ref, coef_ref, range_ref,
     vel_ref, frc_ref, str_ref,
-    rims, rims_turned, edges, slopes, packs, packs_turned,
+    source, turned, sides, far_rim, slopes, packs, packs_turned,
 ):
     f32 = jnp.float32
-
-    def block_row(c, x, y):
-        if y < 2:
-            values = low_ref[c, x, y : y + 1]
-        elif y < 6:
-            values = mid_ref[c, x, y - 2 : y - 1]
-        else:
-            values = high_ref[c, x, y - 6 : y - 5]
-        return values + (x - 2.5, y - 3.5, 0.0)[c]
-
-    for v in range(3):
-        for c in range(3):
-            for x in range(6):
-                for s in range(2):
-                    row = 12 * (3 * v + c) + 2 * x + s
-                    rims[row : row + 1] = block_row(c, x, (1, 6)[s] + v - 1)
-    boxes = []
-    for x in range(6):
-        boxes.append((mid_ref[0, x], mid_ref[2, x]))
-        boxes.append((low_ref[0, x], low_ref[2, x]))
-        boxes.append((high_ref[0, x], high_ref[2, x]))
-    reach = reach_of(boxes)
+    mate_high = side_of_mate()
+    far_high = 1 - mate_high
 
     def coef(k):
         return jnp.broadcast_to(coef_ref[k : k + 1], (8, SLOTS))
@@ -219,50 +286,35 @@
     a = [coef(k) for k in range(4)]
     p = [coef(4 + k) for k in range(4)]
     am = monic(a)
-
-    def rim(ref, u, v, c):
-        start = 12 * (3 * (v + 1) + c) + 2 * (1 + u)
-        return ref[start : start + 8]
-
-    outer = [rim(rims, 0, 0, c) for c in range(3)]
-    for c in range(3):
-        for x in range(4):
-            for s in range(2):
-                edges[c, 2 * x + s : 2 * x + s + 1] = block_row(c, x + 1, (2, 5)[s])
-    inner = [edges[c] for c in range(3)]
-
-    def density_step(d, ref, totals):
-        same = jnp.where(d == 0, 100.0, 0.0)
-        out, inn = totals
-        for u in (-1, 0, 1):
-            for v in (-1, 0, 1):
-                others = [rim(ref, u, v, c) for c in range(3)]
-                square = square_of(outer, others)
-                if u == 0 and v == 0:
-                    square = square + same
-                out = out + density_term(square, am)
-                if v == 0:
-                    inn = inn + density_term(square_of(inner, others), am)
-        return (out, inn)
-
     zero = jnp.zeros((8, SLOTS), f32)
-    out, inn = offsets_loop(reach, rims, rims_turned, density_step, (zero, zero))
-    edges[0] = out
-    edges[1] = inn
+    boxes = [(far_ref[0, x], far_ref[2, x]) for x in range(6)]
+    extent = joined(gap_range(boxes), (range_ref[0:1], range_ref[1:2]))
+    reach = reach_of(*extent)
+    far_rows = (1 - far_high, far_high)
+    rim_density(far_high, mid_ref, far_ref, far_rows, am, extent, source, turned, sides, far_rim)
     for x in range(4):
-        for s in range(2):
-            row = 2 * x + s
-            slopes[6 * x + 5 * s : 6 * x + 5 * s + 1] = edges[0, row : row + 1]
-            mine = 4 * x + 3 * s
-            slopes[6 * x + 3 * s + 1 : 6 * x + 3 * s + 2] = (
-                sum_ref[mine : mine + 1] + edges[1, row : row + 1]
+        slopes[6 * x + 2 : 6 * x + 4] = sum_ref[4 * x + 1 : 4 * x + 3]
+        for high, rim in ((mate_high, rim_ref), (far_high, far_rim)):
+            slopes[pl.ds(6 * x + 5 * high, 1)] = rim[x : x + 1]
+            slopes[pl.ds(6 * x + 1 + 3 * high, 1)] = (
+                sum_ref[pl.ds(4 * x + 3 * high, 1)] + rim[4 + x : 5 + x]
             )
-        slopes[6 * x + 2 : 6 * x + 4] = sum_ref[4 * x + 1 : 4 * x + 3]
     for m in range(3):
         total = slopes[8 * m : 8 * m + 8] * a[3]
         slope = (-0.5 * coef(8)) / jnp.sqrt(1.0 + total) + (2.0 * coef(9)) * total
         slopes[8 * m : 8 * m + 8] = slope * (a[3] / p[3])
 
+    for high, halo, near in (
+        (mate_high, mate_ref, 3 - 3 * mate_high),
+        (far_high, far_ref, far_rows[0]),
+    ):
+        height = (2 * high - 1).astype(f32) * 2.5
+        for u in (-1, 0, 1):
+            for s in range(2):
+                x = 2 + s + u
+                for c in range(3):
+                    values = halo[c, x, pl.ds(near, 1)] + (x - 2.5, height, 0.0)[c]
+                    packs[pl.ds(96 * (u + 1) + 8 * c + 4 * s + 67 * high, 1)] = values
     for u in (-1, 0, 1):
         for v in (-1, 0, 1):
             k = 3 * (u + 1) + v + 1
@@ -270,9 +322,6 @@
                 x = 2 + s + u
                 for c in range(3):
                     base = 8 * (4 * k + c) + 4 * s
-                    for y in range(2 + v, 6 + v):
-                        if y in (1, 6):
-                            packs[base + y - 2 - v : base + y - 1 - v] = block_row(c, x, y)
                     first = max(2, 2 + v)
                     last = min(6, 6 + v)
                     block = mid_ref[c, x, first - 2 : last - 2]
@@ -373,39 +422,52 @@
     early = pl.pallas_call(
         early_kernel,
         in_specs=[smem] * 3 + [vmem],
-        out_specs=[vmem] * 2,
-        out_shape=[jax.ShapeDtypeStruct((16, SLOTS), f32)] * 2,
+        out_specs=[vmem] * 3,
+        out_shape=[jax.ShapeDtypeStruct((r, SLOTS), f32) for r in (16, 16, 8)],
         scratch_shapes=[pltpu.VMEM((216, SLOTS), f32), pltpu.VMEM((2, 216, SLOTS), f32)],
         cost_estimate=pl.CostEstimate(flops=12000000, bytes_accessed=60000, transcendentals=0),
         compiler_params=pltpu.CompilerParams(vmem_limit_bytes=GRANT),
         name="early",
     )
-    total, coefs = early(density_coef, pair_coef, embed_coef, mid)
+    total, coefs, extent = early(density_coef, pair_coef, embed_coef, mid)
     passed = jnp.where(even, mate[:, :, 2:], mate[:, :, :2])
     route = [(i, (i + 2 - 4 * (i % 2)) % count) for i in range(count)]
     far = lax.ppermute(passed, "gy", route)
-    low = jnp.where(even, far, mate[:, :, 2:])
-    high = jnp.where(even, mate[:, :, :2], far)
+    rim_scratch = [
+        pltpu.VMEM((72, SLOTS), f32),
+        pltpu.VMEM((2, 72, SLOTS), f32),
+        pltpu.VMEM((2, 3, 8, SLOTS), f32),
+    ]
+    past_mate = pl.pallas_call(
+        mate_kernel,
+        in_specs=[vmem] * 4,
+        out_specs=[vmem] * 2,
+        out_shape=[jax.ShapeDtypeStruct((8, SLOTS), f32)] * 2,
+        scratch_shapes=rim_scratch,
+        cost_estimate=pl.CostEstimate(flops=5000000, bytes_accessed=60000, transcendentals=0),
+        compiler_params=pltpu.CompilerParams(vmem_limit_bytes=GRANT),
+        name="past_mate",
+    )
+    rim, wide = past_mate(mid, mate, coefs, extent)
     vel, frc, stress = pl.pallas_call(
         late_kernel,
-        in_specs=[vmem] * 7,
+        in_specs=[vmem] * 9,
         out_specs=[vmem] * 3,
         out_shape=[
             jax.ShapeDtypeStruct(flat, f32),
             jax.ShapeDtypeStruct(flat, f32),
             jax.ShapeDtypeStruct((6, 8, SLOTS), f32),
         ],
-        scratch_shapes=[
-            pltpu.VMEM((112, SLOTS), f32),
-            pltpu.VMEM((2, 112, SLOTS), f32),
-            pltpu.VMEM((3, 8, SLOTS), f32),
+        scratch_shapes=rim_scratch
+        + [
+            pltpu.VMEM((8, SLOTS), f32),
             pltpu.VMEM((24, SLOTS), f32),
             pltpu.VMEM((288, SLOTS), f32),
             pltpu.VMEM((2, 288, SLOTS), f32),
         ],
         compiler_params=pltpu.CompilerParams(vmem_limit_bytes=GRANT),
         name="late",
-    )(mid, low, high, half, slot, total, coefs)
+    )(mid, mate, far, half, slot, total, rim, coefs, wide)
     return (
         new.reshape(shape),
         vel.reshape(shape),

time: 52.6 us -> 50.9 us (0.968)
  Pallas kernels: 12.4 us -> 10.7 us
    pallas_call x2 -> x3, Pallas kernels: 10.1 us -> 8.36 us  [the longest x1 4.37 us: body(): pl.pallas_call(late_kernel, in_specs=[vmem] * 9, out_specs=[vmem] * 3, ou...]
  transfers between devices with their start and end apart: 4 -> 4, of which waited for: 2 -> 2; matrix products, arithmetic and copies ran while one was open for 0% -> 0% of each run, Pallas kernels for 7% -> 8%
where the time goes in v5:
time: 50.9 us; the launch traced here: 50.6 us
  starting transfers between devices  27.4 us (54%)
  waiting for transfers between devices  11.7 us (23%)
  Pallas kernels  10.7 us (21%)
  between operations  0.76 us (1%)
    ppermute x2, starting transfers between devices, shifted(): return lax.ppermute(block, axis, route)  19 us
    ppermute x2, waiting for transfers between devices, shifted(): return lax.ppermute(block, axis, route)  6.99 us
    ppermute x1, starting transfers between devices, body(): mate = lax.ppermute(mid, 'gy', swap)  5.04 us
    ppermute x1, waiting for transfers between devices, body(): mate = lax.ppermute(mid, 'gy', swap)  4.7 us
    pallas_call x1, Pallas kernels, body(): pl.pallas_call(late_kernel, in_specs=[vmem] * 9, out_specs=[vmem] * 3, ou...  4.37 us
    ppermute x1, starting transfers between devices, body(): far = lax.ppermute(passed, 'gy', route)  3.4 us
    pallas_call x1, Pallas kernels, body(): total, coefs, extent = early(density_coef, pair_coef, embed_coef, mid)  2.8 us
    pallas_call x1, Pallas kernels, body(): pl.pallas_call(place_kernel, in_specs=[hbm] * 4, out_specs=[vmem] * 4, ou...  2.37 us
  transfers between devices with their start and end apart: 4, of which 2 were waited for; matrix products, arithmetic and copies ran while one was open for 0% of the time, Pallas kernels for 8%

profile of v5, /device:TPU:2, one launch (start us, length us, event | category | flops | bytes accessed | tf_op | source)
XLA Modules:
  0.0 50.6 jit_solution(2804140558890426620)
XLA Ops:
  0.6 2.4 %place.1 = (f32[3,8,128]{2,1,0:T(8,128)}, f32[3,8,128]{2,1,0:T(8,128)S(1)}, f32[3,8,128]{2,1,0:T(8,128)S(1)}, s32[8,128]{1,0:T(8,128)S(1)}) custom-call(s32[2,4]{1,0:T(2,128)} %counts_hbm.1, f32[3,8,128]{2,1,0:T(8,128)} %bitcast.11, f32[3,8,128]{2,1,0:T(8,128)} %bitcast.12, f32[3,8,128]{2,1,0:T(8,128)} %bitcast.13), custom_call_target="tpu_custom_call" | custom-call | tf_op jit(solution)/shard_map/place/pallas_call | solution.py:390
  3.0 17.1 %collective-permute-start.1 = (f32[3,2,4,128]{3,2,1,0:T(4,128)S(1)}, f32[3,2,4,128]{3,2,1,0:T(4,128)S(1)}, u32[]{:S(2)}, u32[]{:S(2)}) collective-permute-start(f32[3,2,4,128]{3,2,1,0:T(4,128)S(1)} %bitcast.8), channel_id=1, source_target_pairs={{0,760},{8,0},{16,8},{24,16},{32,24},{40,32},{48,40},{56,48},{64,5... | collective-permute-start | bytes 36872 | tf_op jit(solution)/shard_map/ppermute | solution.py:380
  20.1 1.9 %collective-permute-start = (f32[3,2,4,128]{3,2,1,0:T(4,128)S(1)}, f32[3,2,4,128]{3,2,1,0:T(4,128)S(1)}, u32[]{:S(2)}, u32[]{:S(2)}) collective-permute-start(f32[3,2,4,128]{3,2,1,0:T(4,128)S(1)} %bitcast.9), channel_id=1, source_target_pairs={{0,8},{8,16},{16,24},{24,32},{32,40},{40,48},{48,56},{56,64},{64,7... | collective-permute-start | bytes 36872 | tf_op jit(solution)/shard_map/ppermute | solution.py:380
  22.0 0.0 collective-permute-done.1
  22.0 7.0 %collective-permute-done = f32[3,2,4,128]{3,2,1,0:T(4,128)S(1)} collective-permute-done((f32[3,2,4,128]{3,2,1,0:T(4,128)S(1)}, f32[3,2,4,128]{3,2,1,0:T(4,128)S(1)}, u32[]{:S(2)}, u32[]{:S(2)}) %collective-permute-start) | collective-permute-done | bytes 12320 | tf_op jit(solution)/shard_map/ppermute | solution.py:380
  29.0 5.0 %collective-permute-start.2 = (f32[3,6,4,128]{3,2,1,0:T(4,128)S(1)}, f32[3,6,4,128]{3,2,1,0:T(4,128)S(1)}, u32[]{:S(2)}, u32[]{:S(2)}) collective-permute-start(f32[3,6,4,128]{3,2,1,0:T(4,128)S(1)} %pad_maximum_fusion.mid_ref), channel_id=1, source_target_pairs={{0,1},{1,0},{2,3},{3,2},{4,5},{5,4},{6,7},{7,6},{8,9},{9,8},{10,11... | collective-permute-start | bytes 110600 | tf_op jit(solution)/shard_map/ppermute | solution.py:421
  34.1 0.0 copy-start
  34.1 0.0 copy-start.1
  34.1 0.0 copy-start.2
  34.1 4.7 %collective-permute-done.2.mate_ref = f32[3,6,4,128]{3,2,1,0:T(4,128)S(1)} collective-permute-done((f32[3,6,4,128]{3,2,1,0:T(4,128)S(1)}, f32[3,6,4,128]{3,2,1,0:T(4,128)S(1)}, u32[]{:S(2)}, u32[]{:S(2)}) %collective-permute-start.2) | collective-permute-done | bytes 36896 | tf_op jit(solution)/shard_map/ppermute | solution.py:421
  38.8 3.4 %collective-permute-start.3 = (f32[3,6,2,128]{3,2,1,0:T(2,128)S(1)}, f32[3,6,2,128]{3,2,1,0:T(2,128)S(1)}, u32[]{:S(2)}, u32[]{:S(2)}) collective-permute-start(f32[3,6,2,128]{3,2,1,0:T(2,128)S(1)} %slice_select_fusion), channel_id=1, source_target_pairs={{0,2},{1,7},{2,4},{3,1},{4,6},{5,3},{6,0},{7,5},{8,10},{9,15},{10,... | collective-permute-start | bytes 55304 | tf_op jit(solution)/shard_map/ppermute | solution.py:435
  42.2 0.0 copy-done
  42.2 0.0 copy-done.1
  42.3 0.0 copy-done.2
  42.3 2.8 %early.1 = (f32[16,128]{1,0:T(8,128)S(1)}, f32[16,128]{1,0:T(8,128)S(1)}, f32[8,128]{1,0:T(8,128)S(1)}) custom-call(f32[4]{0:T(128)S(1)} %copy-done, f32[4]{0:T(128)S(1)} %copy-done.1, f32[2]{0:T(128)S(1)} %copy-done.2, f32[3,6,4,128]{3,2,1,0:T(4,128)S(1)} %pad_maximum_fusion.mid_ref), custom_call_target="tpu_custom_call" | custom-call | flops 12000000 | bytes 60000 | tf_op jit(solution)/shard_map/early/pallas_call | solution.py:432
  45.1 1.2 %past_mate.1 = (f32[8,128]{1,0:T(8,128)S(1)}, f32[8,128]{1,0:T(8,128)S(1)}) custom-call(f32[3,6,4,128]{3,2,1,0:T(4,128)S(1)} %pad_maximum_fusion.mid_ref, f32[3,6,4,128]{3,2,1,0:T(4,128)S(1)} %collective-permute-done.2.mate_ref, f32[16,128]{1,0:T(8,128)S(1)} %get-tuple-element.21.coef_ref, f32[8,128]{1,0:T(8,128)S(1)} %get-tuple-element.22.range_ref), custom_call_target="tpu_custom_call" | custom-call | flops 5000000 | bytes 60000 | tf_op jit(solution)/shard_map/past_mate/pallas_call | solution.py:451
  46.3 0.0 collective-permute-done.3.far_ref
  46.3 4.4 %late.1 = (f32[3,8,128]{2,1,0:T(8,128)}, f32[3,8,128]{2,1,0:T(8,128)}, f32[6,8,128]{2,1,0:T(8,128)}) custom-call(f32[3,6,4,128]{3,2,1,0:T(4,128)S(1)} %pad_maximum_fusion.mid_ref, f32[3,6,4,128]{3,2,1,0:T(4,128)S(1)} %collective-permute-done.2.mate_ref, f32[3,6,2,128]{3,2,1,0:T(2,128)S(1)} %collective-permute-done.3.far_ref, ...), custom_call_target="tpu_custom_call" | custom-call | tf_op jit(solution)/shard_map/late/pallas_call | solution.py:452
  (2 shorter events, 0.0 us)
Async XLA Ops:
  3.0 19.0 %collective-permute-start.1 = (f32[3,2,4,128]{3,2,1,0:T(4,128)S(1)}, f32[3,2,4,128]{3,2,1,0:T(4,128)S(1)}, u32[]{:S(2)}, u32[]{:S(2)}) collective-permute-start(f32[3,2,4,128]{3,2,1,0:T(4,128)S(1)} %bitcast.8), channel_id=1, source_target_pairs={{0,760},{8,0},{16,8},{24,16},{32,24},{40,32},{48,40},{56,48},{64,5... | collective-permute-start | bytes 36872 | tf_op jit(solution)/shard_map/ppermute | solution.py:380
  20.1 8.9 %collective-permute-start = (f32[3,2,4,128]{3,2,1,0:T(4,128)S(1)}, f32[3,2,4,128]{3,2,1,0:T(4,128)S(1)}, u32[]{:S(2)}, u32[]{:S(2)}) collective-permute-start(f32[3,2,4,128]{3,2,1,0:T(4,128)S(1)} %bitcast.9), channel_id=1, source_target_pairs={{0,8},{8,16},{16,24},{24,32},{32,40},{40,48},{48,56},{56,64},{64,7... | collective-permute-start | bytes 36872 | tf_op jit(solution)/shard_map/ppermute | solution.py:380
  29.0 9.8 %collective-permute-start.2 = (f32[3,6,4,128]{3,2,1,0:T(4,128)S(1)}, f32[3,6,4,128]{3,2,1,0:T(4,128)S(1)}, u32[]{:S(2)}, u32[]{:S(2)}) collective-permute-start(f32[3,6,4,128]{3,2,1,0:T(4,128)S(1)} %pad_maximum_fusion.mid_ref), channel_id=1, source_target_pairs={{0,1},{1,0},{2,3},{3,2},{4,5},{5,4},{6,7},{7,6},{8,9},{9,8},{10,11... | collective-permute-start | bytes 110600 | tf_op jit(solution)/shard_map/ppermute | solution.py:421
  34.1 8.2 %copy-start = (f32[4]{0:T(128)S(1)}, f32[4]{0:T(128)}, u32[]{:S(2)}) copy-start(f32[4]{0:T(128)} %dens_ref.1) | copy-start | bytes 52
  34.1 8.2 %copy-start.1 = (f32[4]{0:T(128)S(1)}, f32[4]{0:T(128)}, u32[]{:S(2)}) copy-start(f32[4]{0:T(128)} %pair_ref.1) | copy-start | bytes 52
  34.1 8.2 %copy-start.2 = (f32[2]{0:T(128)S(1)}, f32[2]{0:T(128)}, u32[]{:S(2)}) copy-start(f32[2]{0:T(128)} %emb_ref.1) | copy-start | bytes 28
  38.8 7.4 %collective-permute-start.3 = (f32[3,6,2,128]{3,2,1,0:T(2,128)S(1)}, f32[3,6,2,128]{3,2,1,0:T(2,128)S(1)}, u32[]{:S(2)}, u32[]{:S(2)}) collective-permute-start(f32[3,6,2,128]{3,2,1,0:T(2,128)S(1)} %slice_select_fusion), channel_id=1, source_target_pairs={{0,2},{1,7},{2,4},{3,1},{4,6},{5,3},{6,0},{7,5},{8,10},{9,15},{10,... | collective-permute-start | bytes 55304 | tf_op jit(solution)/shard_map/ppermute | solution.py:435
